TPU v7x, 256 devices: a whole 4x4x8 slice. The times are simulated.
256 devices in a mesh: prow: 16 (over z, core), pcol: 16 (over x, y).
Axes of the slice: x: 4, y: 4, z: 8, core: 2. Of those that a mesh axis runs over, the one named last changes fastest.
Arguments:
- right_side: float32 [7, 4096, 256], P(None, 'prow'), may hold values from -6 to 6
- inverse_diag: float32 [7, 4096, 4096], P(None, 'pcol', 'prow'), as said below
- panels: float32 [7, 16384, 4096], P(None, 'prow', 'pcol'), may hold values from -0.09375 to 0.09375
- block_rows: int32 [7, 128], P(None, 'prow'), may hold values from 128 to 479, as said below
Outputs:
- solution: float32 [7, 4096, 256], P(None, 'pcol')
- upper_update: float32 [32768, 256], P(('prow', 'pcol'))
Inputs may be any that keep to these rules, and one draw needn't show every extreme that they name: inverse_diag[k] is lower triangular with a positive diagonal. block_rows[k, j] is a block row of an ancestor of supernode k or an upper block row, and the entries of one supernode are distinct. The entries j with j // 8 = p lie in blocks p * 2 to (p + 1) * 2 - 1 of an ancestor's rows or in upper block rows p * 16 to (p + 1) * 16 - 1.
All inputs are finite; a program needn't handle non-finite values.
Results may differ from a plain program's by a relative error of at most 0.00011.
Values sent between devices are 32-bit elements; how exact they have to be, the bound alone decides.
A program may use at most 64 MiB of HBM per device.

v0:
```python
import jax
import jax.numpy as jnp
from jax import lax
from jax.sharding import PartitionSpec as P

BLOCK_ROWS = 128
SUPER_BLOCKS = 32
SUPERNODES = 7


LEVELS = ((0, 1, 2, 3), (4, 5), (6,))


def place_terms(targets, products, proc_row, own_blocks, upper_own, count_local):
    windowed = SUPERNODES * SUPER_BLOCKS
    node_of = targets // SUPER_BLOCKS
    local_win = node_of * own_blocks + targets % SUPER_BLOCKS - proc_row * own_blocks
    local_up = SUPERNODES * own_blocks + targets - windowed - proc_row * upper_own
    local_index = jnp.where(targets < windowed, local_win, local_up)
    positions = lax.broadcasted_iota(jnp.int32, (1, count_local, 1), 1)
    onehot = (positions == local_index[:, None, :]).astype(jnp.float32)
    flattened = products.reshape(products.shape[0], targets.shape[1], -1)
    return jnp.einsum("nls,nsx->lx", onehot, flattened, precision=lax.Precision.HIGHEST)


def per_device(right_side, inverse_diag, panels, block_rows):
    rhs_cols = right_side.shape[2]
    own_blocks = right_side.shape[1] // BLOCK_ROWS
    slot_count = block_rows.shape[1]
    upper_own = 2 * slot_count
    win_local = SUPERNODES * own_blocks
    count_local = win_local + upper_own
    row_width = BLOCK_ROWS * rhs_cols
    proc_row = lax.axis_index("prow")
    summed = jnp.zeros((win_local, row_width), jnp.float32)
    upper_rows = upper_own * BLOCK_ROWS // lax.axis_size("pcol")
    upper_part = jnp.zeros((upper_rows, rhs_cols), jnp.float32)
    solved = []
    for level_nodes in LEVELS:
        first_node = level_nodes[0]
        last_node = level_nodes[-1] + 1
        node_count = last_node - first_node
        low_row = first_node * own_blocks
        high_row = last_node * own_blocks
        own_sums = summed[low_row:high_row]
        residual = right_side[first_node:last_node] - own_sums.reshape(
            node_count, own_blocks * BLOCK_ROWS, rhs_cols
        )
        inv_terms = jnp.einsum(
            "nij,njk->nik",
            inverse_diag[first_node:last_node],
            residual,
            precision=lax.Precision.HIGHEST,
        )
        solution = lax.psum(inv_terms, "prow")
        solved.append(solution)
        products = jnp.einsum(
            "nij,njk->nik", panels[first_node:last_node], solution, precision=lax.Precision.HIGHEST
        )
        fresh_sums = place_terms(
            block_rows[first_node:last_node], products, proc_row, own_blocks, upper_own, count_local
        )
        if high_row < win_local:
            later_sums = lax.psum(fresh_sums[high_row:win_local], "pcol")
            summed = jnp.concatenate([summed[:high_row], summed[high_row:] + later_sums], axis=0)
        upper_fresh = fresh_sums[win_local:].reshape(upper_own * BLOCK_ROWS, rhs_cols)
        upper_part = upper_part + lax.psum_scatter(
            upper_fresh, "pcol", scatter_dimension=0, tiled=True
        )
    return (jnp.concatenate(solved, axis=0), upper_part)


def solution(mesh):
    in_specs = (
        P(None, "prow", None),
        P(None, "pcol", "prow"),
        P(None, "prow", "pcol"),
        P(None, "prow"),
    )
    out_specs = (P(None, "pcol", None), P(("prow", "pcol"), None))
    return jax.shard_map(
        per_device, mesh=mesh, in_specs=in_specs, out_specs=out_specs, check_vma=False
    )
```

profile of v0, /device:TPU:1, one launch (start us, length us, event | category | flops | bytes accessed | tf_op | source)
XLA Modules:
  0.0 680.5 jit_solution(751858983523541049)
XLA Ops:
  7.2 3.7 fusion.12
  11.0 115.3 %all-reduce.6.cloned.1.call-done = f32[4,256,256]{2,1,0:T(8,128)} async-done(((f32[4,256,256]{2,1,0:T(8,128)}), f32[4,256,256]{2,1,0:T(8,128)}) %all-reduce.6.cloned.1.call-update) | async-done | bytes 1048592 | tf_op jit(solution)/shard_map/psum | solution.py:55
  126.3 11.2 %fusion.2 = f32[4,1024,256]{1,2,0:T(8,128)} fusion(f32[4,256,256]{2,1,0:T(8,128)} %all-reduce.6.cloned.1.call-done, f32[7,1024,256]{2,1,0:T(8,128)} %param.6), kind=kOutput, calls=%fused_computation.5 | convolution fusion | flops 3221225472 | bytes 9437184 | tf_op jit(solution)/shard_map/nij,njk->nik/dot_general | solution.py:57
  137.5 5.4 copy.12
  142.9 5.0 reshape.123
  147.8 4.0 convolution_bitcast_fusion.1
  151.8 1.9 copy-done
  154.9 96.2 %all-reduce.8.cloned.1.call-done = f32[6,32768]{1,0:T(8,128)} async-done(((f32[6,32768]{1,0:T(8,128)}), f32[6,32768]{1,0:T(8,128)}) %all-reduce.8.cloned.1.call-update) | async-done | bytes 786448 | tf_op jit(solution)/shard_map/psum | solution.py:64
  252.7 2.7 convolution_bitcast_fusion.3
  255.7 110.1 %all-reduce.10.cloned.1.call-done = f32[2,256,256]{2,1,0:T(8,128)} async-done(((f32[2,256,256]{2,1,0:T(8,128)}), f32[2,256,256]{2,1,0:T(8,128)}) %all-reduce.10.cloned.1.call-update) | async-done | bytes 524304 | tf_op jit(solution)/shard_map/psum | solution.py:55
  365.7 5.2 fusion.7
  371.0 1.8 copy.16
  372.8 1.7 reshape.125
  374.6 2.0 convolution_bitcast_fusion
  376.6 2.0 copy-done.1
  379.4 93.5 %all-reduce.12.cloned.1.call-done = f32[2,32768]{1,0:T(2,128)} async-done(((f32[2,32768]{1,0:T(2,128)}), f32[2,32768]{1,0:T(2,128)}) %all-reduce.12.cloned.1.call-update) | async-done | bytes 262160 | tf_op jit(solution)/shard_map/psum | solution.py:64
  472.9 1.5 slice_add_fusion.1
  474.7 2.1 convolution_bitcast_fusion.4
  476.9 109.2 %all-reduce.14.cloned.1.call-done = f32[1,256,256]{2,1,0:T(8,128)} async-done(((f32[1,256,256]{2,1,0:T(8,128)}), f32[1,256,256]{2,1,0:T(8,128)}) %all-reduce.14.cloned.1.call-update) | async-done | bytes 262160 | tf_op jit(solution)/shard_map/psum | solution.py:55
  586.1 3.2 convolution_bitcast_fusion.2
  589.8 4.1 convolution_add_fusion
  593.9 1.5 reshape.136
  596.8 1.4 pad_maximum_fusion
  598.2 75.5 %reduce-scatter.2.cloned.1.call-done = f32[128,256]{1,0:T(8,128)} async-done(((f32[2048,256]{1,0:T(8,128)}), f32[128,256]{1,0:T(8,128)}) %reduce-scatter.2.cloned.1.call-update) | async-done | bytes 131088 | tf_op jit(solution)/shard_map/reduce_scatter | solution.py:67
  (33 shorter events, 6.3 us)
Async XLA Ops:
  7.2 3.8 copy-start.5
  7.2 119.1 %all-reduce.6.cloned.1.call-start = ((), (), s32[]{:S(2)}) async-start(), calls=%async_computation.1 | async-start | bytes 2097152 | tf_op jit(solution)/shard_map/psum | solution.py:55
  10.9 240.2 %all-reduce.8.cloned.1.call-start = ((), (), s32[]{:S(2)}) async-start(), calls=%async_computation.2 | async-start | bytes 2097152 | tf_op jit(solution)/shard_map/psum | solution.py:64
  151.8 1.9 copy-start
  154.8 210.9 %all-reduce.10.cloned.1.call-start = ((), (), s32[]{:S(2)}) async-start(), calls=%async_computation.3 | async-start | bytes 1048576 | tf_op jit(solution)/shard_map/psum | solution.py:55
  255.4 217.5 %all-reduce.12.cloned.1.call-start = ((), (), s32[]{:S(2)}) async-start(), calls=%async_computation.4 | async-start | bytes 524288 | tf_op jit(solution)/shard_map/psum | solution.py:64
  376.6 2.0 copy-start.1
  379.4 206.7 %all-reduce.14.cloned.1.call-start = ((), (), s32[]{:S(2)}) async-start(), calls=%async_computation.5 | async-start | bytes 524288 | tf_op jit(solution)/shard_map/psum | solution.py:55
  476.8 196.8 %reduce-scatter.2.cloned.1.call-start = ((), (), s32[]{:S(2)}) async-start(), calls=%async_computation.6 | async-start | bytes 2228224 | tf_op jit(solution)/shard_map/reduce_scatter | solution.py:67
  595.4 1.2 copy-start.2
  595.4 1.4 copy-start.3
  595.4 1.4 copy-start.4
Sparse Core Ops, SparseCore 0:
  11.0 115.1 all-reduce.5
  155.0 96.0 all-reduce.7
  255.6 110.1 all-reduce.9
  379.5 93.3 all-reduce.11
  477.0 109.0 all-reduce.13
  595.6 78.0 reduce-scatter.1
where the time goes:
time: 681 us
  waiting for transfers between devices  600 us (88%)
  matrix products  38.1 us (6%)
  local copies, waits for them, and re-layouts  25.1 us (4%)
  between operations  14.3 us (2%)
    psum x3, waiting for transfers between devices, per_device(): solution = lax.psum(inv_terms, 'prow')  334 us
    psum x2, waiting for transfers between devices, per_device(): later_sums = lax.psum(fresh_sums[high_row:win_local], 'pcol')  190 us
    reduce_scatter x1, waiting for transfers between devices, per_device(): lax.psum_scatter(upper_fresh, 'pcol', scatter_dimension=0, tiled=True)  75.5 us
    dot_general x3, matrix products, per_device(): jnp.einsum('nij,njk->nik', panels[first_node:last_node], solution, precis...  19.6 us
  transfers between devices with their start and end apart: 6, of which 6 were waited for; matrix products, arithmetic and copies ran while one was open for 0% of the time, Pallas kernels for 0%

commit v1 on v0

v1 whole, which is shorter than its diff:
```python
import functools

import jax
import jax.numpy as jnp
from jax import lax
from jax.experimental import pallas as pl
from jax.experimental.pallas import tpu as pltpu
from jax.sharding import PartitionSpec as P

BLOCK_ROWS = 128
SUPER_BLOCKS = 32
SUPERNODES = 7
LEVELS = ((0, 4), (4, 2), (6, 1))
MESH = pl.DeviceIdType.MESH
F32 = jnp.float32
BF16 = jnp.bfloat16


def split(value):
    high = value.astype(BF16)
    low = (value - high.astype(F32)).astype(BF16)
    return high, low


def dot3(a_high, a_low, b_high, b_low):
    dot = functools.partial(jnp.dot, preferred_element_type=F32)
    return dot(a_high, b_high) + (dot(a_high, b_low) + dot(a_low, b_high))


def wait_bytes(ref, sem):
    pltpu.make_async_copy(ref, ref, sem).wait()


def kernel(
    chips, cols, inv_ref, rhs_hbm, diag_hbm, panel_hbm, sol_hbm, up_hbm,
    rhs, diag, panel, panel_high, panel_low, terms, pair_in, half, ring_in, xs, prod,
    win0, win1, win_in0, win_in1, res, piece0, piece1, upper, upper_in, up_out,
    load_sem, panel_sem, pair_send, pair_recv, ring_send, ring_recv, gather_send, gather_recv,
    share_send, share_recv, win_send, win_recv, back_send, back_recv, up_send, up_recv, out_sem,
):
    prow = lax.axis_index("prow")
    pcol = lax.axis_index("pcol")
    chip, core = prow // 2, prow % 2
    other = chip * 2 + 1 - core
    own_half, other_half = core * BLOCK_ROWS, (1 - core) * BLOCK_ROWS
    rows = BLOCK_ROWS // chips
    own_rows = own_half + chip * rows

    loads = []
    for level, (first, count) in enumerate(LEVELS):
        nodes = pl.ds(first, count)
        loads.append((
            pltpu.make_async_copy(rhs_hbm.at[nodes], rhs.at[nodes], load_sem.at[2 * level]),
            pltpu.make_async_copy(diag_hbm.at[nodes], diag.at[nodes], load_sem.at[2 * level + 1]),
        ))
    for pair in loads:
        for copy in pair:
            copy.start()
    panel_loads = [
        pltpu.make_async_copy(panel_hbm.at[k], panel.at[k], panel_sem.at[k]) for k in range(SUPERNODES)
    ]
    for copy in panel_loads:
        copy.start()

    barrier = pltpu.get_barrier_semaphore()
    pl.semaphore_signal(barrier, inc=1, device_id=(other, pcol), device_id_type=MESH)

    def greet_chip(i, carry):
        peer = lax.rem(chip + i, chips) * 2 + core
        pl.semaphore_signal(barrier, inc=1, device_id=(peer, pcol), device_id_type=MESH)
        return carry

    def greet_col(i, carry):
        pl.semaphore_signal(
            barrier, inc=1, device_id=(prow, lax.rem(pcol + i, cols)), device_id_type=MESH
        )
        return carry

    lax.fori_loop(1, chips, greet_chip, 0)
    lax.fori_loop(1, cols, greet_col, 0)
    pl.semaphore_wait(barrier, chips + cols - 1)

    def solve_terms(node, residual):
        d_high, d_low = split(diag[node])
        r_high, r_low = split(residual)
        terms[node] = dot3(d_high, d_low, r_high, r_low)
        pltpu.make_async_remote_copy(
            src_ref=terms.at[node, pl.ds(other_half, BLOCK_ROWS)], dst_ref=pair_in.at[node],
            send_sem=pair_send.at[node], recv_sem=pair_recv.at[node],
            device_id=(other, pcol), device_id_type=MESH,
        ).start()

    def scatter_half(node, carry):
        wait_bytes(pair_in.at[node], pair_recv.at[node])
        half[node] = terms[node, pl.ds(own_half, BLOCK_ROWS)] + pair_in[node]

        def send(i, inner):
            peer = lax.rem(chip + i, chips)
            pltpu.make_async_remote_copy(
                src_ref=half.at[node, pl.ds(peer * rows, rows)], dst_ref=ring_in.at[node, i],
                send_sem=ring_send.at[node], recv_sem=ring_recv.at[node],
                device_id=(peer * 2 + core, pcol), device_id_type=MESH,
            ).start()
            return inner

        lax.fori_loop(1, chips, send, 0)
        return carry

    def gather_half(node, carry):
        wait_bytes(ring_in.at[node, pl.ds(1, chips - 1)], ring_recv.at[node])
        total = half[node, pl.ds(chip * rows, rows)]
        for i in range(1, chips):
            total = total + ring_in[node, i]
        xs[node, pl.ds(own_rows, rows)] = total

        def send(i, inner):
            peer = lax.rem(chip + i, chips)
            pltpu.make_async_remote_copy(
                src_ref=xs.at[node, pl.ds(own_rows, rows)], dst_ref=xs.at[node, pl.ds(own_rows, rows)],
                send_sem=gather_send.at[node], recv_sem=gather_recv.at[node],
                device_id=(peer * 2 + core, pcol), device_id_type=MESH,
            ).start()
            return inner

        lax.fori_loop(1, chips, send, 0)
        return carry

    def share_half(node, carry):
        wait_bytes(ring_in.at[node, pl.ds(1, chips - 1)], gather_recv.at[node])
        pltpu.make_async_remote_copy(
            src_ref=xs.at[node, pl.ds(own_half, BLOCK_ROWS)],
            dst_ref=xs.at[node, pl.ds(own_half, BLOCK_ROWS)],
            send_sem=share_send.at[node], recv_sem=share_recv.at[node],
            device_id=(other, pcol), device_id_type=MESH,
        ).start()
        return carry

    def multiply(node, carry):
        wait_bytes(xs.at[node, pl.ds(other_half, BLOCK_ROWS)], share_recv.at[node])
        x_high, x_low = split(xs[node])

        def quarter(b, inner):
            part = pl.ds(b * 256, 256)
            product = dot3(panel_high[node, part], panel_low[node, part], x_high, x_low)
            prod[node, 2 * b] = product[:BLOCK_ROWS]
            prod[node, 2 * b + 1] = product[BLOCK_ROWS:]
            return inner

        lax.fori_loop(0, 4, quarter, 0)
        return carry

    def split_panels(first, count):
        for node in range(first, first + count):
            panel_loads[node].wait()

        def one(step, carry):
            node, part = first + step // 8, pl.ds((step % 8) * BLOCK_ROWS, BLOCK_ROWS)
            high, low = split(panel[node, part])
            panel_high[node, part] = high
            panel_low[node, part] = low
            return carry

        lax.fori_loop(0, 8 * count, one, 0)

    def solve_level(level, residual_of, between):
        first, count = LEVELS[level]
        for copy in loads[level]:
            copy.wait()

        def begin(node, carry):
            solve_terms(node, residual_of(node))
            return carry

        lax.fori_loop(first, first + count, begin, 0)
        lax.fori_loop(first, first + count, scatter_half, 0)
        between()
        lax.fori_loop(first, first + count, gather_half, 0)
        lax.fori_loop(first, first + count, share_half, 0)
        lax.fori_loop(first, first + count, multiply, 0)

    def picked(node, dest):
        return prod[node, inv_ref[node, dest]]

    def add_upper(first, count, fresh):
        def one(j, carry):
            total = picked(first, 6 + j)
            for node in range(first + 1, first + count):
                total = total + picked(node, 6 + j)
            upper[j] = total if fresh else upper[j] + total
            return carry

        lax.fori_loop(0, upper.shape[0], one, 0)

    def reduce_window(which, win, win_in, piece, first):
        size = win.shape[0] // cols

        def send(i, carry):
            peer = lax.rem(pcol + i, cols)
            pltpu.make_async_remote_copy(
                src_ref=win.at[pl.ds(peer * size, size)], dst_ref=win_in.at[i],
                send_sem=win_send.at[which], recv_sem=win_recv.at[which],
                device_id=(prow, peer), device_id_type=MESH,
            ).start()
            return carry

        lax.fori_loop(1, cols, send, 0)

        def finish():
            wait_bytes(win_in.at[pl.ds(1, cols - 1)], win_recv.at[which])
            total = win[pl.ds(pcol * size, size)]
            for i in range(1, cols):
                total = total + win_in[i]
            begin = first * 2 * BLOCK_ROWS + pcol * size
            node, row = begin // (2 * BLOCK_ROWS), begin % (2 * BLOCK_ROWS)
            here = res.at[node - 4, pl.ds(row, size)]
            res[node - 4, pl.ds(row, size)] = rhs[node, pl.ds(row, size)] - total

            def spread(i, carry):
                pltpu.make_async_remote_copy(
                    src_ref=here, dst_ref=here,
                    send_sem=back_send.at[which], recv_sem=back_recv.at[which],
                    device_id=(prow, lax.rem(pcol + i, cols)), device_id_type=MESH,
                ).start()
                return carry

            lax.fori_loop(1, cols, spread, 0)
            wait_bytes(win_in.at[pl.ds(1, cols - 1)], back_recv.at[which])

        return finish

    def store_solution(level):
        first, count = LEVELS[level]
        nodes = pl.ds(first, count)
        copy = pltpu.make_async_copy(xs.at[nodes], sol_hbm.at[nodes], out_sem.at[level])
        copy.start()
        return copy

    def prepare():
        def clear(node, carry):
            prod[node, 8] = jnp.zeros((BLOCK_ROWS, prod.shape[3]), F32)
            return carry

        lax.fori_loop(0, SUPERNODES, clear, 0)
        split_panels(0, 4)

    solve_level(0, lambda node: rhs[node], prepare)
    stores = [store_solution(0)]
    for j in range(4):
        child = 2 * (j // 2)
        win0[pl.ds(j * BLOCK_ROWS, BLOCK_ROWS)] = picked(child, j) + picked(child + 1, j)
    finish = reduce_window(0, win0, win_in0, piece0, 4)
    add_upper(0, 4, True)
    for copy in loads[1]:
        copy.wait()
    loads[1] = ()
    finish()

    solve_level(1, lambda node: res[node - 4], lambda: split_panels(4, 2))
    stores.append(store_solution(1))
    for j in range(2):
        total = picked(0, 4 + j)
        for node in range(1, 6):
            total = total + picked(node, 4 + j)
        win1[pl.ds(j * BLOCK_ROWS, BLOCK_ROWS)] = total
    finish = reduce_window(1, win1, win_in1, piece1, 6)
    add_upper(4, 2, False)
    for copy in loads[2]:
        copy.wait()
    loads[2] = ()
    finish()

    solve_level(2, lambda node: res[node - 4], lambda: split_panels(6, 1))
    stores.append(store_solution(2))
    add_upper(6, 1, False)
    size = upper.shape[0] // cols

    def send_upper(i, carry):
        peer = lax.rem(pcol + i, cols)
        pltpu.make_async_remote_copy(
            src_ref=upper.at[pl.ds(peer * size, size)], dst_ref=upper_in.at[i],
            send_sem=up_send, recv_sem=up_recv, device_id=(prow, peer), device_id_type=MESH,
        ).start()
        return carry

    lax.fori_loop(1, cols, send_upper, 0)
    wait_bytes(upper_in.at[pl.ds(1, cols - 1)], up_recv)

    for b in range(size):
        def sum_rows(t, carry):
            part = pl.ds(t * 32, 32)
            total = upper[pcol * size + b, part]
            for i in range(1, cols):
                total = total + upper_in[i, b, part]
            up_out[b, part] = total
            return carry

        lax.fori_loop(0, BLOCK_ROWS // 32, sum_rows, 0)
    last = pltpu.make_async_copy(up_out, up_hbm, out_sem.at[3])
    last.start()

    def drain(node, carry):
        wait_bytes(pair_in.at[node], pair_send.at[node])
        wait_bytes(ring_in.at[node, pl.ds(1, chips - 1)], ring_send.at[node])
        wait_bytes(ring_in.at[node, pl.ds(1, chips - 1)], gather_send.at[node])
        wait_bytes(pair_in.at[node], share_send.at[node])
        return carry

    lax.fori_loop(0, SUPERNODES, drain, 0)
    for which, win_in in enumerate((win_in0, win_in1)):
        wait_bytes(win_in.at[pl.ds(1, cols - 1)], win_send.at[which])
        wait_bytes(win_in.at[pl.ds(1, cols - 1)], back_send.at[which])
    wait_bytes(upper_in.at[pl.ds(1, cols - 1)], up_send)
    for copy in stores:
        copy.wait()
    last.wait()


def inverse_map(block_rows, own_blocks, upper_own, super_blocks):
    proc_row = lax.axis_index("prow")
    windowed = SUPERNODES * super_blocks
    node_of = block_rows // super_blocks
    local_win = (node_of - 4) * own_blocks + block_rows % super_blocks - proc_row * own_blocks
    local_up = 3 * own_blocks + block_rows - windowed - proc_row * upper_own
    local = jnp.where(block_rows < windowed, local_win, local_up)
    slots = block_rows.shape[1]
    dest = lax.broadcasted_iota(jnp.int32, (1, 3 * own_blocks + upper_own, 1), 1)
    slot = lax.broadcasted_iota(jnp.int32, (1, 1, slots), 2)
    return jnp.min(jnp.where(dest == local[:, None, :], slot, slots), axis=2)


def per_device(chips, cols, super_blocks, right_side, inverse_diag, panels, block_rows):
    rhs_cols = right_side.shape[2]
    order = right_side.shape[1]
    own_blocks = order // BLOCK_ROWS
    upper_own = 2 * block_rows.shape[1]
    inverse = inverse_map(block_rows, own_blocks, upper_own, super_blocks)
    rows = BLOCK_ROWS // chips
    win_rows = (4 * BLOCK_ROWS, 2 * BLOCK_ROWS)
    size = upper_own // cols
    dma = pltpu.SemaphoreType.DMA
    scratch = [
        pltpu.VMEM((7, order, rhs_cols), F32),
        pltpu.VMEM((7, order, order), F32),
        pltpu.VMEM(panels.shape, F32),
        pltpu.VMEM(panels.shape, BF16),
        pltpu.VMEM(panels.shape, BF16),
        pltpu.VMEM((7, order, rhs_cols), F32),
        pltpu.VMEM((7, BLOCK_ROWS, rhs_cols), F32),
        pltpu.VMEM((7, BLOCK_ROWS, rhs_cols), F32),
        pltpu.VMEM((7, chips, rows, rhs_cols), F32),
        pltpu.VMEM((7, order, rhs_cols), F32),
        pltpu.VMEM((7, 9, BLOCK_ROWS, rhs_cols), F32),
        pltpu.VMEM((win_rows[0], rhs_cols), F32),
        pltpu.VMEM((win_rows[1], rhs_cols), F32),
        pltpu.VMEM((cols, win_rows[0] // cols, rhs_cols), F32),
        pltpu.VMEM((cols, win_rows[1] // cols, rhs_cols), F32),
        pltpu.VMEM((3, order, rhs_cols), F32),
        pltpu.VMEM((8, rhs_cols), F32),
        pltpu.VMEM((8, rhs_cols), F32),
        pltpu.VMEM((upper_own, BLOCK_ROWS, rhs_cols), F32),
        pltpu.VMEM((cols, size, BLOCK_ROWS, rhs_cols), F32),
        pltpu.VMEM((size, BLOCK_ROWS, rhs_cols), F32),
        dma((6,)), dma((7,)),
        dma((7,)), dma((7,)), dma((7,)), dma((7,)), dma((7,)), dma((7,)),
        dma((7,)), dma((7,)), dma((2,)), dma((2,)), dma((2,)), dma((2,)),
        dma, dma, dma((4,)),
    ]
    anywhere = pl.BlockSpec(memory_space=pl.ANY)
    solved, upper = pl.pallas_call(
        functools.partial(kernel, chips, cols),
        out_shape=(
            jax.ShapeDtypeStruct((7, order, rhs_cols), F32),
            jax.ShapeDtypeStruct((size, BLOCK_ROWS, rhs_cols), F32),
        ),
        in_specs=[pl.BlockSpec(memory_space=pltpu.SMEM), anywhere, anywhere, anywhere],
        out_specs=(anywhere, anywhere),
        scratch_shapes=scratch,
        compiler_params=pltpu.CompilerParams(
            collective_id=0, has_side_effects=True, vmem_limit_bytes=56 * 1024 * 1024
        ),
    )(inverse, right_side, inverse_diag, panels)
    return solved, upper.reshape(size * BLOCK_ROWS, rhs_cols)


def solution(mesh):
    chips, cols = mesh.shape["prow"] // 2, mesh.shape["pcol"]
    super_blocks = 2 * mesh.shape["prow"]
    in_specs = (
        P(None, "prow", None),
        P(None, "pcol", "prow"),
        P(None, "prow", "pcol"),
        P(None, "prow"),
    )
    out_specs = (P(None, "pcol", None), P(("prow", "pcol"), None))
    return jax.shard_map(
        functools.partial(per_device, chips, cols, super_blocks),
        mesh=mesh, in_specs=in_specs, out_specs=out_specs, check_vma=False,
    )
```

time: 681 us -> 158 us (0.23)
  the two profiles are of different devices: /device:TPU:1 before, /device:TPU:93 now
where the time goes in v1:
time: 158 us
  Pallas kernels  152 us (96%)
  local copies, waits for them, and re-layouts  3.6 us (2%)
    pallas_call x1, Pallas kernels, per_device(): pl.pallas_call(functools.partial(kernel, chips, cols), out_shape=(jax.Sha...  152 us
    unnamed x4, local copies, waits for them, and re-layouts  3.6 us

profile of v1, /device:TPU:93, one launch (start us, length us, event | category | flops | bytes accessed | tf_op | source)
XLA Modules:
  0.0 158.0 jit_solution(10023905667248346428)
XLA Ops:
  0.6 0.7 fusion.4
  1.3 0.7 select_reduce_fusion.inv_ref
  2.0 152.4 %shard_map.59 = (f32[7,256,256]{2,1,0:T(8,128)}, f32[1,128,256]{2,1,0:T(8,128)}) custom-call(s32[7,22]{1,0:T(8,128)} %select_reduce_fusion.inv_ref, f32[7,256,256]{2,1,0:T(8,128)} %rhs_hbm.1, f32[7,256,256]{2,1,0:T(8,128)} %diag_hbm.1, f32[7,1024,256]{2,1,0:T(8,128)} %panel_hbm.1), custom_call_target="tpu_custom_call" | custom-call | tf_op jit(solution)/shard_map/pallas_call | solution.py:369
  154.4 0.0 copy-start
  154.4 2.9 %copy.8 = f32[7,256,256]{2,1,0:T(8,128)} copy(f32[7,256,256]{2,1,0:T(8,128)} %get-tuple-element.8) | data formatting | bytes 3670016
  157.4 0.0 copy-done
  157.4 0.7 copy.9
Async XLA Ops:
  154.4 3.0 %copy-start = (f32[1,128,256]{2,1,0:T(8,128)S(1)}, f32[1,128,256]{2,1,0:T(8,128)}, u32[]{:S(2)}) copy-start(f32[1,128,256]{2,1,0:T(8,128)} %get-tuple-element.5) | copy-start | bytes 393220

commit v2 on v1

v2 whole, which is shorter than its diff:
```python
import functools
import math

import jax
import jax.numpy as jnp
from jax import lax
from jax.experimental import pallas as pl
from jax.experimental.pallas import tpu as pltpu
from jax.sharding import PartitionSpec as P

BLOCK_ROWS = 128
SUPER_BLOCKS = 32
SUPERNODES = 7
MESH = pl.DeviceIdType.MESH
F32 = jnp.float32
BF16 = jnp.bfloat16


def split(value):
    high = value.astype(BF16)
    low = (value - high.astype(F32)).astype(BF16)
    return high, low


def dot3(a_high, a_low, b_high, b_low):
    dot = functools.partial(jnp.dot, preferred_element_type=F32)
    return dot(a_high, b_high) + (dot(a_high, b_low) + dot(a_low, b_high))


def wait_bytes(ref, sem):
    pltpu.make_async_copy(ref, ref, sem).wait()


def kernel(
    chips, side, inv_ref, rhs_hbm, diag_hbm, panel_hbm, sol_hbm, up_hbm,
    rhs, diag, panel, panel_high, panel_low, terms, pair_in, half, ring_in, xs, prod,
    win, win_in, res, upper, up_in, up_mid, up_last, up_out,
    rhs_sem, diag_sem, panel_sem, pair_send, pair_recv, ring_send, ring_recv,
    gather_send, gather_recv, share_send, share_recv, win_send, win_recv, back_send, back_recv,
    up_send, up_recv, last_send, last_recv, out_sem,
):
    cols = side * side
    prow = lax.axis_index("prow")
    pcol = lax.axis_index("pcol")
    chip, core = prow // 2, prow % 2
    col_x, col_y = pcol // side, pcol % side
    other = chip * 2 + 1 - core
    own_half, other_half = core * BLOCK_ROWS, (1 - core) * BLOCK_ROWS
    rows = BLOCK_ROWS // chips
    own_rows = own_half + chip * rows
    sent = []

    loads = {}
    for k in range(SUPERNODES):
        loads["rhs", k] = pltpu.make_async_copy(rhs_hbm.at[k], rhs.at[k], rhs_sem.at[k])
        loads["diag", k] = pltpu.make_async_copy(diag_hbm.at[k], diag.at[k], diag_sem.at[k])
        loads["panel", k] = pltpu.make_async_copy(panel_hbm.at[k], panel.at[k], panel_sem.at[k])
    for k in range(4):
        loads["rhs", k].start()
        loads["diag", k].start()
    for k in range(SUPERNODES):
        if k >= 4:
            loads["rhs", k].start()
            loads["diag", k].start()
        loads["panel", k].start()

    barrier = pltpu.get_barrier_semaphore()
    pl.semaphore_signal(barrier, inc=1, device_id=(other, pcol), device_id_type=MESH)

    def greet_chip(i, carry):
        peer = lax.rem(chip + i, chips) * 2 + core
        pl.semaphore_signal(barrier, inc=1, device_id=(peer, pcol), device_id_type=MESH)
        return carry

    def greet_col(i, carry):
        pl.semaphore_signal(
            barrier, inc=1, device_id=(prow, lax.rem(pcol + i, cols)), device_id_type=MESH
        )
        return carry

    lax.fori_loop(1, chips, greet_chip, 0)
    lax.fori_loop(1, cols, greet_col, 0)

    def begin_node(node, residual):
        d_high, d_low = split(diag[node])
        r_high, r_low = split(residual[...])
        terms[node] = dot3(d_high, d_low, r_high, r_low)

    def pair_node(node):
        pltpu.make_async_remote_copy(
            src_ref=terms.at[node, pl.ds(other_half, BLOCK_ROWS)], dst_ref=pair_in.at[node],
            send_sem=pair_send.at[node], recv_sem=pair_recv.at[node],
            device_id=(other, pcol), device_id_type=MESH,
        ).start()
        sent.append((pair_in.at[node], pair_send.at[node]))

    def scatter_node(node):
        wait_bytes(pair_in.at[node], pair_recv.at[node])
        half[node] = terms[node, pl.ds(own_half, BLOCK_ROWS)] + pair_in[node]

        def send(i, inner):
            peer = lax.rem(chip + i, chips)
            pltpu.make_async_remote_copy(
                src_ref=half.at[node, pl.ds(peer * rows, rows)], dst_ref=ring_in.at[node, i],
                send_sem=ring_send.at[node], recv_sem=ring_recv.at[node],
                device_id=(peer * 2 + core, pcol), device_id_type=MESH,
            ).start()
            return inner

        lax.fori_loop(1, chips, send, 0)
        sent.append((ring_in.at[node, pl.ds(1, chips - 1)], ring_send.at[node]))

    def gather_node(node):
        wait_bytes(ring_in.at[node, pl.ds(1, chips - 1)], ring_recv.at[node])
        total = half[node, pl.ds(chip * rows, rows)]
        for i in range(1, chips):
            total = total + ring_in[node, i]
        xs[node, pl.ds(own_rows, rows)] = total
        here = xs.at[node, pl.ds(own_rows, rows)]

        def send(i, inner):
            peer = lax.rem(chip + i, chips)
            pltpu.make_async_remote_copy(
                src_ref=here, dst_ref=here,
                send_sem=gather_send.at[node], recv_sem=gather_recv.at[node],
                device_id=(peer * 2 + core, pcol), device_id_type=MESH,
            ).start()
            return inner

        lax.fori_loop(1, chips, send, 0)
        sent.append((ring_in.at[node, pl.ds(1, chips - 1)], gather_send.at[node]))

    def share_node(node):
        wait_bytes(ring_in.at[node, pl.ds(1, chips - 1)], gather_recv.at[node])
        here = xs.at[node, pl.ds(own_half, BLOCK_ROWS)]
        pltpu.make_async_remote_copy(
            src_ref=here, dst_ref=here,
            send_sem=share_send.at[node], recv_sem=share_recv.at[node],
            device_id=(other, pcol), device_id_type=MESH,
        ).start()
        sent.append((pair_in.at[node], share_send.at[node]))

    def multiply_node(node):
        wait_bytes(xs.at[node, pl.ds(other_half, BLOCK_ROWS)], share_recv.at[node])
        x_high, x_low = split(xs[node])

        def quarter(b, inner):
            part = pl.ds(b * 256, 256)
            product = dot3(panel_high[node, part], panel_low[node, part], x_high, x_low)
            prod[node, 2 * b] = product[:BLOCK_ROWS]
            prod[node, 2 * b + 1] = product[BLOCK_ROWS:]
            return inner

        lax.fori_loop(0, 4, quarter, 0)

    def store_node(node):
        copy = pltpu.make_async_copy(xs.at[node], sol_hbm.at[node], out_sem.at[node])
        copy.start()
        return copy

    def split_panel(node):
        loads["panel", node].wait()

        def one(step, carry):
            part = pl.ds(step * BLOCK_ROWS, BLOCK_ROWS)
            panel_high[node, part], panel_low[node, part] = split(panel[node, part])
            return carry

        lax.fori_loop(0, 8, one, 0)

    def picked(node, dest):
        return prod[node, inv_ref[node, dest]]

    size = 2 * BLOCK_ROWS // cols

    def send_window(target, nodes):
        which = target - 4
        for b in range(2):
            total = picked(nodes[0], 2 * which + b)
            for node in nodes[1:]:
                total = total + picked(node, 2 * which + b)
            win[which, pl.ds(b * BLOCK_ROWS, BLOCK_ROWS)] = total

        def send(i, carry):
            peer = lax.rem(pcol + i, cols)
            pltpu.make_async_remote_copy(
                src_ref=win.at[which, pl.ds(peer * size, size)], dst_ref=win_in.at[which, i],
                send_sem=win_send.at[which], recv_sem=win_recv.at[which],
                device_id=(prow, peer), device_id_type=MESH,
            ).start()
            return carry

        lax.fori_loop(1, cols, send, 0)
        sent.append((win_in.at[which, pl.ds(1, cols - 1)], win_send.at[which]))

    def spread_window(target):
        which = target - 4
        loads["rhs", target].wait()
        wait_bytes(win_in.at[which, pl.ds(1, cols - 1)], win_recv.at[which])
        mine = pl.ds(pcol * size, size)
        total = win[which, mine]
        for i in range(1, cols):
            total = total + win_in[which, i]
        res[which, mine] = rhs[target, mine] - total
        here = res.at[which, mine]

        def spread(i, carry):
            pltpu.make_async_remote_copy(
                src_ref=here, dst_ref=here,
                send_sem=back_send.at[which], recv_sem=back_recv.at[which],
                device_id=(prow, lax.rem(pcol + i, cols)), device_id_type=MESH,
            ).start()
            return carry

        lax.fori_loop(1, cols, spread, 0)
        sent.append((win_in.at[which, pl.ds(1, cols - 1)], back_send.at[which]))

    def begin_parent(target):
        which = target - 4
        loads["diag", target].wait()
        wait_bytes(win_in.at[which, pl.ds(1, cols - 1)], back_recv.at[which])
        begin_node(target, res.at[which])
        pair_node(target)

    def add_upper(which, nodes, fresh):
        count = upper.shape[3] // BLOCK_ROWS

        def one(j, carry):
            total = picked(nodes[0], 6 + j)
            for node in nodes[1:]:
                total = total + picked(node, 6 + j)
            place = j // count
            part = pl.ds((j % count) * BLOCK_ROWS, BLOCK_ROWS)
            spot = (which, place // side, place % side, part)
            upper[spot] = total if fresh else upper[spot] + total
            return carry

        lax.fori_loop(0, cols * count, one, 0)

    up_rows = upper.shape[3] // 2
    first_rows, second_rows = pl.ds(0, up_rows), pl.ds(up_rows, up_rows)

    def send_upper(which):
        for i in range(1, side):
            peer_x, peer_y = lax.rem(col_x + i, side), lax.rem(col_y + i, side)
            pltpu.make_async_remote_copy(
                src_ref=upper.at[which, peer_x, :, first_rows], dst_ref=up_in.at[which, 0, i],
                send_sem=up_send.at[which, 0], recv_sem=up_recv.at[which, 0],
                device_id=(prow, peer_x * side + col_y), device_id_type=MESH,
            ).start()
            pltpu.make_async_remote_copy(
                src_ref=upper.at[which, :, peer_y, second_rows], dst_ref=up_in.at[which, 1, i],
                send_sem=up_send.at[which, 1], recv_sem=up_recv.at[which, 1],
                device_id=(prow, col_x * side + peer_y), device_id_type=MESH,
            ).start()
        for way in range(2):
            sent.append((up_in.at[which, way, pl.ds(1, side - 1)], up_send.at[which, way]))

    def middle_upper(which):
        for way in range(2):
            wait_bytes(up_in.at[which, way, pl.ds(1, side - 1)], up_recv.at[which, way])

            def one(j, carry):
                if way == 0:
                    total = upper[which, col_x, j, first_rows]
                else:
                    total = upper[which, j, col_y, second_rows]
                for i in range(1, side):
                    total = total + up_in[which, way, i, j]
                up_mid[which, way, j] = total
                return carry

            lax.fori_loop(0, side, one, 0)
            for i in range(1, side):
                if way == 0:
                    place = lax.rem(col_y + i, side)
                    peer = col_x * side + place
                else:
                    place = lax.rem(col_x + i, side)
                    peer = place * side + col_y
                pltpu.make_async_remote_copy(
                    src_ref=up_mid.at[which, way, place], dst_ref=up_last.at[which, way, i],
                    send_sem=last_send.at[which, way], recv_sem=last_recv.at[which, way],
                    device_id=(prow, peer), device_id_type=MESH,
                ).start()
            sent.append((up_last.at[which, way, pl.ds(1, side - 1)], last_send.at[which, way]))

    def finish_upper(which, fresh):
        for way in range(2):
            wait_bytes(up_last.at[which, way, pl.ds(1, side - 1)], last_recv.at[which, way])
            total = up_mid[which, way, col_y if way == 0 else col_x]
            for i in range(1, side):
                total = total + up_last[which, way, i]
            part = first_rows if way == 0 else second_rows
            up_out[part] = total if fresh else up_out[part] + total

    def run():
        for node in range(4):
            loads["rhs", node].wait()
            loads["diag", node].wait()
            begin_node(node, rhs.at[node])
            if node == 0:
                pl.semaphore_wait(barrier, chips + cols - 1)
            pair_node(node)
        yield
        for node in range(4):
            scatter_node(node)
        for node in range(SUPERNODES):
            prod[node, 8] = jnp.zeros((BLOCK_ROWS, prod.shape[3]), F32)
        for node in range(2):
            split_panel(node)
        yield
        for node in range(4):
            gather_node(node)
        for node in range(2, 4):
            split_panel(node)
        yield
        for parent in (4, 5):
            children = (2 * parent - 8, 2 * parent - 7)
            for node in children:
                share_node(node)
            for node in children:
                multiply_node(node)
            send_window(parent, children)
            yield
        for node in range(4, 7):
            split_panel(node)
        spread_window(4)
        spread_window(5)
        yield
        stores = [store_node(node) for node in range(4)]
        add_upper(0, (0, 1, 2, 3), True)
        begin_parent(4)
        begin_parent(5)
        yield
        scatter_node(4)
        scatter_node(5)
        gather_node(4)
        gather_node(5)
        yield
        share_node(4)
        share_node(5)
        multiply_node(4)
        multiply_node(5)
        send_window(6, (0, 1, 2, 3, 4, 5))
        yield
        stores += [store_node(node) for node in (4, 5)]
        add_upper(0, (4, 5), False)
        spread_window(6)
        send_upper(0)
        yield
        begin_parent(6)
        scatter_node(6)
        gather_node(6)
        yield
        middle_upper(0)
        share_node(6)
        multiply_node(6)
        yield
        add_upper(1, (6,), True)
        send_upper(1)
        stores.append(store_node(6))
        finish_upper(0, True)
        middle_upper(1)
        yield
        finish_upper(1, False)
        last = pltpu.make_async_copy(up_out, up_hbm, out_sem.at[7])
        last.start()
        for copy in stores:
            copy.wait()
        last.wait()

    for _ in run():
        pass
    for ref, sem in sent:
        wait_bytes(ref, sem)


def inverse_map(block_rows, own_blocks, upper_own, super_blocks):
    proc_row = lax.axis_index("prow")
    windowed = SUPERNODES * super_blocks
    node_of = block_rows // super_blocks
    local_win = (node_of - 4) * own_blocks + block_rows % super_blocks - proc_row * own_blocks
    local_up = 3 * own_blocks + block_rows - windowed - proc_row * upper_own
    local = jnp.where(block_rows < windowed, local_win, local_up)
    slots = block_rows.shape[1]
    dest = lax.broadcasted_iota(jnp.int32, (1, 3 * own_blocks + upper_own, 1), 1)
    slot = lax.broadcasted_iota(jnp.int32, (1, 1, slots), 2)
    return jnp.min(jnp.where(dest == local[:, None, :], slot, slots), axis=2)


def per_device(chips, side, super_blocks, right_side, inverse_diag, panels, block_rows):
    rhs_cols = right_side.shape[2]
    order = right_side.shape[1]
    own_blocks = order // BLOCK_ROWS
    upper_own = 2 * block_rows.shape[1]
    inverse = inverse_map(block_rows, own_blocks, upper_own, super_blocks)
    rows = BLOCK_ROWS // chips
    cols = side * side
    own_upper = upper_own * BLOCK_ROWS // cols
    dma = pltpu.SemaphoreType.DMA
    scratch = [
        pltpu.VMEM((7, order, rhs_cols), F32),
        pltpu.VMEM((7, order, order), F32),
        pltpu.VMEM(panels.shape, F32),
        pltpu.VMEM(panels.shape, BF16),
        pltpu.VMEM(panels.shape, BF16),
        pltpu.VMEM((7, order, rhs_cols), F32),
        pltpu.VMEM((7, BLOCK_ROWS, rhs_cols), F32),
        pltpu.VMEM((7, BLOCK_ROWS, rhs_cols), F32),
        pltpu.VMEM((7, chips, rows, rhs_cols), F32),
        pltpu.VMEM((7, order, rhs_cols), F32),
        pltpu.VMEM((7, 9, BLOCK_ROWS, rhs_cols), F32),
        pltpu.VMEM((3, order, rhs_cols), F32),
        pltpu.VMEM((3, cols, order // cols, rhs_cols), F32),
        pltpu.VMEM((3, order, rhs_cols), F32),
        pltpu.VMEM((2, side, side, own_upper, rhs_cols), F32),
        pltpu.VMEM((2, 2, side, side, own_upper // 2, rhs_cols), F32),
        pltpu.VMEM((2, 2, side, own_upper // 2, rhs_cols), F32),
        pltpu.VMEM((2, 2, side, own_upper // 2, rhs_cols), F32),
        pltpu.VMEM((own_upper, rhs_cols), F32),
        dma((7,)), dma((7,)), dma((7,)), dma((7,)), dma((7,)), dma((7,)), dma((7,)),
        dma((7,)), dma((7,)), dma((7,)), dma((7,)), dma((3,)), dma((3,)), dma((3,)), dma((3,)),
        dma((2, 2)), dma((2, 2)), dma((2, 2)), dma((2, 2)), dma((8,)),
    ]
    anywhere = pl.BlockSpec(memory_space=pl.ANY)
    return pl.pallas_call(
        functools.partial(kernel, chips, side),
        out_shape=(
            jax.ShapeDtypeStruct((7, order, rhs_cols), F32),
            jax.ShapeDtypeStruct((own_upper, rhs_cols), F32),
        ),
        in_specs=[pl.BlockSpec(memory_space=pltpu.SMEM), anywhere, anywhere, anywhere],
        out_specs=(anywhere, anywhere),
        scratch_shapes=scratch,
        compiler_params=pltpu.CompilerParams(
            collective_id=0, has_side_effects=True, vmem_limit_bytes=58 * 1024 * 1024
        ),
    )(inverse, right_side, inverse_diag, panels)


def solution(mesh):
    chips, side = mesh.shape["prow"] // 2, math.isqrt(mesh.shape["pcol"])
    super_blocks = 2 * mesh.shape["prow"]
    in_specs = (
        P(None, "prow", None),
        P(None, "pcol", "prow"),
        P(None, "prow", "pcol"),
        P(None, "prow"),
    )
    out_specs = (P(None, "pcol", None), P(("prow", "pcol"), None))
    return jax.shard_map(
        functools.partial(per_device, chips, side, super_blocks),
        mesh=mesh, in_specs=in_specs, out_specs=out_specs, check_vma=False,
    )
```

time: 158 us -> 132 us (0.84)
  the two profiles are of different devices: /device:TPU:93 before, /device:TPU:1 now
where the time goes in v2:
time: 132 us; the launch traced here: 131 us
  Pallas kernels  126 us (95%)
  local copies, waits for them, and re-layouts  3.6 us (3%)
  other arithmetic  1.39 us (1%)
    pallas_call x1, Pallas kernels, per_device(): pl.pallas_call(functools.partial(kernel, chips, side), out_shape=(jax.Sha...  126 us
    unnamed x4, local copies, waits for them, and re-layouts  3.6 us

profile of v2, /device:TPU:1, one launch (start us, length us, event | category | flops | bytes accessed | tf_op | source)
XLA Modules:
  0.0 131.3 jit_solution(12106669673539524581)
XLA Ops:
  0.6 0.7 fusion.4
  1.3 0.7 select_reduce_fusion.inv_ref
  2.0 125.6 %shard_map.59 = (f32[7,256,256]{2,1,0:T(8,128)}, f32[128,256]{1,0:T(8,128)}) custom-call(s32[7,22]{1,0:T(8,128)} %select_reduce_fusion.inv_ref, f32[7,256,256]{2,1,0:T(8,128)} %rhs_hbm.1, f32[7,256,256]{2,1,0:T(8,128)} %diag_hbm.1, f32[7,1024,256]{2,1,0:T(8,128)} %panel_hbm.1), custom_call_target="tpu_custom_call" | custom-call | tf_op jit(solution)/shard_map/pallas_call | solution.py:427
  127.7 0.0 copy-start
  127.7 2.9 %copy.8 = f32[7,256,256]{2,1,0:T(8,128)} copy(f32[7,256,256]{2,1,0:T(8,128)} %get-tuple-element.4) | data formatting | bytes 3670016
  130.6 0.0 copy-done
  130.6 0.7 copy.9
Async XLA Ops:
  127.7 3.0 %copy-start = (f32[128,256]{1,0:T(8,128)S(1)}, f32[128,256]{1,0:T(8,128)}, u32[]{:S(2)}) copy-start(f32[128,256]{1,0:T(8,128)} %get-tuple-element.5) | copy-start | bytes 393220

commit v3 on v2

--- a/solution.py
+++ b/solution.py
@@ -32,7 +32,7 @@
 
 
 def kernel(
-    chips, side, inv_ref, rhs_hbm, diag_hbm, panel_hbm, sol_hbm, up_hbm,
+    chips, side, super_blocks, rows_ref, rhs_hbm, diag_hbm, panel_hbm, sol_hbm, up_hbm,
     rhs, diag, panel, panel_high, panel_low, terms, pair_in, half, ring_in, xs, prod,
     win, win_in, res, upper, up_in, up_mid, up_last, up_out,
     rhs_sem, diag_sem, panel_sem, pair_send, pair_recv, ring_send, ring_recv,
@@ -50,6 +50,23 @@
     own_rows = own_half + chip * rows
     sent = []
 
+    barrier = pltpu.get_barrier_semaphore()
+    pl.semaphore_signal(barrier, inc=1, device_id=(other, pcol), device_id_type=MESH)
+
+    def greet_chip(i, carry):
+        peer = lax.rem(chip + i, chips) * 2 + core
+        pl.semaphore_signal(barrier, inc=1, device_id=(peer, pcol), device_id_type=MESH)
+        return carry
+
+    def greet_col(i, carry):
+        pl.semaphore_signal(
+            barrier, inc=1, device_id=(prow, lax.rem(pcol + i, cols)), device_id_type=MESH
+        )
+        return carry
+
+    lax.fori_loop(1, chips, greet_chip, 0)
+    lax.fori_loop(1, cols, greet_col, 0)
+
     loads = {}
     for k in range(SUPERNODES):
         loads["rhs", k] = pltpu.make_async_copy(rhs_hbm.at[k], rhs.at[k], rhs_sem.at[k])
@@ -64,23 +81,6 @@
             loads["diag", k].start()
         loads["panel", k].start()
 
-    barrier = pltpu.get_barrier_semaphore()
-    pl.semaphore_signal(barrier, inc=1, device_id=(other, pcol), device_id_type=MESH)
-
-    def greet_chip(i, carry):
-        peer = lax.rem(chip + i, chips) * 2 + core
-        pl.semaphore_signal(barrier, inc=1, device_id=(peer, pcol), device_id_type=MESH)
-        return carry
-
-    def greet_col(i, carry):
-        pl.semaphore_signal(
-            barrier, inc=1, device_id=(prow, lax.rem(pcol + i, cols)), device_id_type=MESH
-        )
-        return carry
-
-    lax.fori_loop(1, chips, greet_chip, 0)
-    lax.fori_loop(1, cols, greet_col, 0)
-
     def begin_node(node, residual):
         d_high, d_low = split(diag[node])
         r_high, r_low = split(residual[...])
@@ -144,14 +144,9 @@
         wait_bytes(xs.at[node, pl.ds(other_half, BLOCK_ROWS)], share_recv.at[node])
         x_high, x_low = split(xs[node])
 
-        def quarter(b, inner):
-            part = pl.ds(b * 256, 256)
-            product = dot3(panel_high[node, part], panel_low[node, part], x_high, x_low)
-            prod[node, 2 * b] = product[:BLOCK_ROWS]
-            prod[node, 2 * b + 1] = product[BLOCK_ROWS:]
-            return inner
-
-        lax.fori_loop(0, 4, quarter, 0)
+        product = dot3(panel_high[node], panel_low[node], x_high, x_low)
+        for slot in range(8):
+            prod[node, slot] = product[slot * BLOCK_ROWS:(slot + 1) * BLOCK_ROWS]
 
     def store_node(node):
         copy = pltpu.make_async_copy(xs.at[node], sol_hbm.at[node], out_sem.at[node])
@@ -168,17 +163,21 @@
 
         lax.fori_loop(0, 8, one, 0)
 
-    def picked(node, dest):
-        return prod[node, inv_ref[node, dest]]
+    def picked(node, block):
+        slot = 8
+        for i in range(8):
+            slot = jnp.where(rows_ref[node, i] == block, i, slot)
+        return prod[node, slot]
 
     size = 2 * BLOCK_ROWS // cols
 
     def send_window(target, nodes):
         which = target - 4
         for b in range(2):
-            total = picked(nodes[0], 2 * which + b)
+            block = target * super_blocks + prow * 2 + b
+            total = picked(nodes[0], block)
             for node in nodes[1:]:
-                total = total + picked(node, 2 * which + b)
+                total = total + picked(node, block)
             win[which, pl.ds(b * BLOCK_ROWS, BLOCK_ROWS)] = total
 
         def send(i, carry):
@@ -226,9 +225,10 @@
         count = upper.shape[3] // BLOCK_ROWS
 
         def one(j, carry):
-            total = picked(nodes[0], 6 + j)
+            block = SUPERNODES * super_blocks + prow * 16 + j
+            total = picked(nodes[0], block)
             for node in nodes[1:]:
-                total = total + picked(node, 6 + j)
+                total = total + picked(node, block)
             place = j // count
             part = pl.ds((j % count) * BLOCK_ROWS, BLOCK_ROWS)
             spot = (which, place // side, place % side, part)
@@ -238,36 +238,41 @@
         lax.fori_loop(0, cols * count, one, 0)
 
     up_rows = upper.shape[3] // 2
-    first_rows, second_rows = pl.ds(0, up_rows), pl.ds(up_rows, up_rows)
-
-    def send_upper(which):
+    chunks = 2
+    piece = up_rows // chunks
+    chunk_of = [pl.ds(i * piece, piece) for i in range(2 * chunks)]
+
+    def send_upper(which, chunk):
         for i in range(1, side):
             peer_x, peer_y = lax.rem(col_x + i, side), lax.rem(col_y + i, side)
             pltpu.make_async_remote_copy(
-                src_ref=upper.at[which, peer_x, :, first_rows], dst_ref=up_in.at[which, 0, i],
-                send_sem=up_send.at[which, 0], recv_sem=up_recv.at[which, 0],
+                src_ref=upper.at[which, peer_x, :, chunk_of[chunk]],
+                dst_ref=up_in.at[which, 0, i, :, chunk_of[chunk]],
+                send_sem=up_send.at[which, 0, chunk], recv_sem=up_recv.at[which, 0, chunk],
                 device_id=(prow, peer_x * side + col_y), device_id_type=MESH,
             ).start()
             pltpu.make_async_remote_copy(
-                src_ref=upper.at[which, :, peer_y, second_rows], dst_ref=up_in.at[which, 1, i],
-                send_sem=up_send.at[which, 1], recv_sem=up_recv.at[which, 1],
+                src_ref=upper.at[which, :, peer_y, chunk_of[chunks + chunk]],
+                dst_ref=up_in.at[which, 1, i, :, chunk_of[chunk]],
+                send_sem=up_send.at[which, 1, chunk], recv_sem=up_recv.at[which, 1, chunk],
                 device_id=(prow, col_x * side + peer_y), device_id_type=MESH,
             ).start()
         for way in range(2):
-            sent.append((up_in.at[which, way, pl.ds(1, side - 1)], up_send.at[which, way]))
-
-    def middle_upper(which):
+            sent.append((up_in.at[which, way, pl.ds(1, side - 1), :, chunk_of[chunk]], up_send.at[which, way, chunk]))
+
+    def middle_upper(which, chunk):
+        part = chunk_of[chunk]
         for way in range(2):
-            wait_bytes(up_in.at[which, way, pl.ds(1, side - 1)], up_recv.at[which, way])
+            wait_bytes(up_in.at[which, way, pl.ds(1, side - 1), :, part], up_recv.at[which, way, chunk])
 
             def one(j, carry):
                 if way == 0:
-                    total = upper[which, col_x, j, first_rows]
+                    total = upper[which, col_x, j, chunk_of[chunk]]
                 else:
-                    total = upper[which, j, col_y, second_rows]
+                    total = upper[which, j, col_y, chunk_of[chunks + chunk]]
                 for i in range(1, side):
-                    total = total + up_in[which, way, i, j]
-                up_mid[which, way, j] = total
+                    total = total + up_in[which, way, i, j, part]
+                up_mid[which, way, j, part] = total
                 return carry
 
             lax.fori_loop(0, side, one, 0)
@@ -279,20 +284,21 @@
                     place = lax.rem(col_x + i, side)
                     peer = place * side + col_y
                 pltpu.make_async_remote_copy(
-                    src_ref=up_mid.at[which, way, place], dst_ref=up_last.at[which, way, i],
-                    send_sem=last_send.at[which, way], recv_sem=last_recv.at[which, way],
+                    src_ref=up_mid.at[which, way, place, part], dst_ref=up_last.at[which, way, i, part],
+                    send_sem=last_send.at[which, way, chunk], recv_sem=last_recv.at[which, way, chunk],
                     device_id=(prow, peer), device_id_type=MESH,
                 ).start()
-            sent.append((up_last.at[which, way, pl.ds(1, side - 1)], last_send.at[which, way]))
-
-    def finish_upper(which, fresh):
+            sent.append((up_last.at[which, way, pl.ds(1, side - 1), part], last_send.at[which, way, chunk]))
+
+    def finish_upper(which, chunk, fresh):
+        part = chunk_of[chunk]
         for way in range(2):
-            wait_bytes(up_last.at[which, way, pl.ds(1, side - 1)], last_recv.at[which, way])
-            total = up_mid[which, way, col_y if way == 0 else col_x]
+            wait_bytes(up_last.at[which, way, pl.ds(1, side - 1), part], last_recv.at[which, way, chunk])
+            total = up_mid[which, way, col_y if way == 0 else col_x, part]
             for i in range(1, side):
-                total = total + up_last[which, way, i]
-            part = first_rows if way == 0 else second_rows
-            up_out[part] = total if fresh else up_out[part] + total
+                total = total + up_last[which, way, i, part]
+            goal = chunk_of[way * chunks + chunk]
+            up_out[goal] = total if fresh else up_out[goal] + total
 
     def run():
         for node in range(4):
@@ -307,13 +313,11 @@
             scatter_node(node)
         for node in range(SUPERNODES):
             prod[node, 8] = jnp.zeros((BLOCK_ROWS, prod.shape[3]), F32)
-        for node in range(2):
+        for node in range(SUPERNODES):
             split_panel(node)
         yield
         for node in range(4):
             gather_node(node)
-        for node in range(2, 4):
-            split_panel(node)
         yield
         for parent in (4, 5):
             children = (2 * parent - 8, 2 * parent - 7)
@@ -323,8 +327,6 @@
                 multiply_node(node)
             send_window(parent, children)
             yield
-        for node in range(4, 7):
-            split_panel(node)
         spread_window(4)
         spread_window(5)
         yield
@@ -335,6 +337,8 @@
         yield
         scatter_node(4)
         scatter_node(5)
+        for chunk in range(chunks):
+            send_upper(0, chunk)
         gather_node(4)
         gather_node(5)
         yield
@@ -345,25 +349,27 @@
         send_window(6, (0, 1, 2, 3, 4, 5))
         yield
         stores += [store_node(node) for node in (4, 5)]
-        add_upper(0, (4, 5), False)
+        add_upper(1, (4, 5), True)
         spread_window(6)
-        send_upper(0)
-        yield
         begin_parent(6)
         scatter_node(6)
+        for chunk in range(chunks):
+            middle_upper(0, chunk)
         gather_node(6)
         yield
-        middle_upper(0)
         share_node(6)
         multiply_node(6)
-        yield
-        add_upper(1, (6,), True)
-        send_upper(1)
+        add_upper(1, (6,), False)
+        for chunk in range(chunks):
+            send_upper(1, chunk)
+        yield
         stores.append(store_node(6))
-        finish_upper(0, True)
-        middle_upper(1)
-        yield
-        finish_upper(1, False)
+        for chunk in range(chunks):
+            finish_upper(0, chunk, True)
+        for chunk in range(chunks):
+            middle_upper(1, chunk)
+        for chunk in range(chunks):
+            finish_upper(1, chunk, False)
         last = pltpu.make_async_copy(up_out, up_hbm, out_sem.at[7])
         last.start()
         for copy in stores:
@@ -376,25 +382,21 @@
         wait_bytes(ref, sem)
 
 
-def inverse_map(block_rows, own_blocks, upper_own, super_blocks):
-    proc_row = lax.axis_index("prow")
-    windowed = SUPERNODES * super_blocks
-    node_of = block_rows // super_blocks
-    local_win = (node_of - 4) * own_blocks + block_rows % super_blocks - proc_row * own_blocks
-    local_up = 3 * own_blocks + block_rows - windowed - proc_row * upper_own
-    local = jnp.where(block_rows < windowed, local_win, local_up)
-    slots = block_rows.shape[1]
-    dest = lax.broadcasted_iota(jnp.int32, (1, 3 * own_blocks + upper_own, 1), 1)
-    slot = lax.broadcasted_iota(jnp.int32, (1, 1, slots), 2)
-    return jnp.min(jnp.where(dest == local[:, None, :], slot, slots), axis=2)
+def copy_out(sol_ref, up_ref, sol_out, up_out, sems):
+    copies = [
+        pltpu.make_async_copy(sol_ref.at[k], sol_out.at[k], sems.at[k]) for k in range(SUPERNODES)
+    ]
+    copies.append(pltpu.make_async_copy(up_ref, up_out, sems.at[SUPERNODES]))
+    for copy in copies:
+        copy.start()
+    for copy in copies:
+        copy.wait()
 
 
 def per_device(chips, side, super_blocks, right_side, inverse_diag, panels, block_rows):
     rhs_cols = right_side.shape[2]
     order = right_side.shape[1]
-    own_blocks = order // BLOCK_ROWS
     upper_own = 2 * block_rows.shape[1]
-    inverse = inverse_map(block_rows, own_blocks, upper_own, super_blocks)
     rows = BLOCK_ROWS // chips
     cols = side * side
     own_upper = upper_own * BLOCK_ROWS // cols
@@ -421,22 +423,30 @@
         pltpu.VMEM((own_upper, rhs_cols), F32),
         dma((7,)), dma((7,)), dma((7,)), dma((7,)), dma((7,)), dma((7,)), dma((7,)),
         dma((7,)), dma((7,)), dma((7,)), dma((7,)), dma((3,)), dma((3,)), dma((3,)), dma((3,)),
-        dma((2, 2)), dma((2, 2)), dma((2, 2)), dma((2, 2)), dma((8,)),
+        dma((2, 2, 2)), dma((2, 2, 2)), dma((2, 2, 2)), dma((2, 2, 2)), dma((8,)),
     ]
     anywhere = pl.BlockSpec(memory_space=pl.ANY)
-    return pl.pallas_call(
-        functools.partial(kernel, chips, side),
-        out_shape=(
-            jax.ShapeDtypeStruct((7, order, rhs_cols), F32),
-            jax.ShapeDtypeStruct((own_upper, rhs_cols), F32),
-        ),
+    shapes = (
+        jax.ShapeDtypeStruct((7, order, rhs_cols), F32),
+        jax.ShapeDtypeStruct((own_upper, rhs_cols), F32),
+    )
+    results = pl.pallas_call(
+        functools.partial(kernel, chips, side, super_blocks),
+        out_shape=shapes,
         in_specs=[pl.BlockSpec(memory_space=pltpu.SMEM), anywhere, anywhere, anywhere],
         out_specs=(anywhere, anywhere),
         scratch_shapes=scratch,
         compiler_params=pltpu.CompilerParams(
             collective_id=0, has_side_effects=True, vmem_limit_bytes=58 * 1024 * 1024
         ),
-    )(inverse, right_side, inverse_diag, panels)
+    )(block_rows, right_side, inverse_diag, panels)
+    return pl.pallas_call(
+        copy_out,
+        out_shape=shapes,
+        in_specs=[anywhere, anywhere],
+        out_specs=(anywhere, anywhere),
+        scratch_shapes=[dma((8,))],
+    )(*results)
 
 
 def solution(mesh):

time: 132 us -> 182 us (1.38)
  Pallas kernels: 126 us -> 181 us
  local copies, waits for them, and re-layouts: 3.6 us -> 0 us
    pallas_call x1 -> x2, Pallas kernels: 126 us -> 181 us  [the longest x1 120 us: per_device(): pl.pallas_call(functools.partial(kernel, chips, side, super_blocks), out_...]
    unnamed x4 -> x0, local copies, waits for them, and re-layouts: 3.6 us -> none
where the time goes in v3:
time: 182 us
  Pallas kernels  181 us (99%)
    pallas_call x1, Pallas kernels, per_device(): pl.pallas_call(functools.partial(kernel, chips, side, super_blocks), out_...  120 us
    pallas_call x1, Pallas kernels, per_device(): pl.pallas_call(copy_out, out_shape=shapes, in_specs=[anywhere, anywhere],...  60.7 us

profile of v3, /device:TPU:1, one launch (start us, length us, event | category | flops | bytes accessed | tf_op | source)
XLA Modules:
  0.0 181.8 jit_solution(13274917978479655129)
XLA Ops:
  0.6 120.4 %shard_map.59 = (f32[7,256,256]{2,1,0:T(8,128)}, f32[128,256]{1,0:T(8,128)}) custom-call(s32[7,8]{1,0:T(8,128)} %rows_ref.1, f32[7,256,256]{2,1,0:T(8,128)} %rhs_hbm.1, f32[7,256,256]{2,1,0:T(8,128)} %diag_hbm.1, f32[7,1024,256]{2,1,0:T(8,128)} %panel_hbm.1), custom_call_target="tpu_custom_call" | custom-call | tf_op jit(solution)/shard_map/pallas_call | solution.py:433
  121.1 60.7 %shard_map.60 = (f32[7,256,256]{2,1,0:T(8,128)}, f32[128,256]{1,0:T(8,128)}) custom-call(f32[7,256,256]{2,1,0:T(8,128)} %get-tuple-element.4.sol_ref, f32[128,256]{1,0:T(8,128)} %get-tuple-element.5.up_ref), custom_call_target="tpu_custom_call" | custom-call | tf_op jit(solution)/shard_map/pallas_call | solution.py:443

commit v4 on v3

--- a/solution.py
+++ b/solution.py
@@ -426,6 +426,7 @@
         dma((2, 2, 2)), dma((2, 2, 2)), dma((2, 2, 2)), dma((2, 2, 2)), dma((8,)),
     ]
     anywhere = pl.BlockSpec(memory_space=pl.ANY)
+    stay = pl.BlockSpec(memory_space=pltpu.HBM)
     shapes = (
         jax.ShapeDtypeStruct((7, order, rhs_cols), F32),
         jax.ShapeDtypeStruct((own_upper, rhs_cols), F32),
@@ -433,19 +434,20 @@
     results = pl.pallas_call(
         functools.partial(kernel, chips, side, super_blocks),
         out_shape=shapes,
-        in_specs=[pl.BlockSpec(memory_space=pltpu.SMEM), anywhere, anywhere, anywhere],
+        in_specs=[pl.BlockSpec(memory_space=pltpu.SMEM), stay, stay, stay],
         out_specs=(anywhere, anywhere),
         scratch_shapes=scratch,
         compiler_params=pltpu.CompilerParams(
-            collective_id=0, has_side_effects=True, vmem_limit_bytes=58 * 1024 * 1024
+            collective_id=0, has_side_effects=True, vmem_limit_bytes=52 * 1024 * 1024
         ),
     )(block_rows, right_side, inverse_diag, panels)
     return pl.pallas_call(
         copy_out,
         out_shape=shapes,
-        in_specs=[anywhere, anywhere],
-        out_specs=(anywhere, anywhere),
+        in_specs=[pl.BlockSpec(memory_space=pltpu.VMEM)] * 2,
+        out_specs=(stay, stay),
         scratch_shapes=[dma((8,))],
+        compiler_params=pltpu.CompilerParams(vmem_limit_bytes=8 * 1024 * 1024),
     )(*results)
 
 

time: 182 us -> 123 us (0.68)
  Pallas kernels: 181 us -> 121 us
    pallas_call x1, Pallas kernels: 60.7 us -> 1.33 us  [per_device(): pl.pallas_call(copy_out, out_shape=shapes, in_specs=[pl.BlockSpec(memory_...]
where the time goes in v4:
time: 123 us; the launch traced here: 122 us
  Pallas kernels  121 us (98%)
    pallas_call x1, Pallas kernels, per_device(): pl.pallas_call(functools.partial(kernel, chips, side, super_blocks), out_...  120 us

profile of v4, /device:TPU:1, one launch (start us, length us, event | category | flops | bytes accessed | tf_op | source)
XLA Modules:
  0.0 122.4 jit_solution(16399819047958976794)
XLA Ops:
  0.6 0.0 copy-start
  0.6 0.7 copy-done
  1.3 119.8 %shard_map.59 = (f32[7,256,256]{2,1,0:T(8,128)S(1)}, f32[128,256]{1,0:T(8,128)S(1)}) custom-call(s32[7,8]{1,0:T(8,128)S(1)} %copy-done, f32[7,256,256]{2,1,0:T(8,128)} %rhs_hbm.1, f32[7,256,256]{2,1,0:T(8,128)} %diag_hbm.1, f32[7,1024,256]{2,1,0:T(8,128)} %panel_hbm.1), custom_call_target="tpu_custom_call" | custom-call | tf_op jit(solution)/shard_map/pallas_call | solution.py:434
  121.1 1.3 %shard_map.60 = (f32[7,256,256]{2,1,0:T(8,128)}, f32[128,256]{1,0:T(8,128)}) custom-call(f32[7,256,256]{2,1,0:T(8,128)S(1)} %get-tuple-element.4.sol_ref, f32[128,256]{1,0:T(8,128)S(1)} %get-tuple-element.5.up_ref), custom_call_target="tpu_custom_call" | custom-call | tf_op jit(solution)/shard_map/pallas_call | solution.py:444
Async XLA Ops:
  0.6 0.7 copy-start

commit v5 on v4

v5 whole, which is shorter than its diff:
```python
import functools
import math

import jax
import jax.numpy as jnp
from jax import lax
from jax.experimental import pallas as pl
from jax.experimental.pallas import tpu as pltpu
from jax.sharding import PartitionSpec as P

BLOCK_ROWS = 128
SUPER_BLOCKS = 32
SUPERNODES = 7
LEVELS = ((0, 4), (4, 2), (6, 1))
MESH = pl.DeviceIdType.MESH
F32 = jnp.float32
BF16 = jnp.bfloat16


def split(value):
    high = value.astype(BF16)
    low = (value - high.astype(F32)).astype(BF16)
    return high, low


def dot3(a_high, a_low, b_high, b_low):
    dot = functools.partial(jnp.dot, preferred_element_type=F32)
    return dot(a_high, b_high) + (dot(a_high, b_low) + dot(a_low, b_high))


def wait_bytes(ref, sem):
    pltpu.make_async_copy(ref, ref, sem).wait()


def kernel(
    chips, side, super_blocks, rows_ref, rhs_hbm, diag_hbm, panel_hbm, sol_hbm, up_hbm,
    rhs, diag, diag_high, diag_low, panel, panel_high, panel_low, terms, pair_in, half, ring_in, xs,
    prod, win, win_in, res, upper, up_in, up_mid, up_last, up_out,
    rhs_sem, diag_sem, panel_sem, pair_send, pair_recv, ring_send, ring_recv,
    gather_send, gather_recv, share_send, share_recv, win_send, win_recv, back_send, back_recv,
    up_send, up_recv, last_send, last_recv, out_sem,
):
    cols = side * side
    width = rhs.shape[3]
    prow = lax.axis_index("prow")
    pcol = lax.axis_index("pcol")
    chip, core = prow // 2, prow % 2
    col_x, col_y = pcol // side, pcol % side
    other = chip * 2 + 1 - core
    own_half, other_half = core * BLOCK_ROWS, (1 - core) * BLOCK_ROWS
    rows = BLOCK_ROWS // chips
    own_rows = own_half + chip * rows
    sent = []

    barrier = pltpu.get_barrier_semaphore()
    pl.semaphore_signal(barrier, inc=1, device_id=(other, pcol), device_id_type=MESH)

    def greet_chip(i, carry):
        peer = lax.rem(chip + i, chips) * 2 + core
        pl.semaphore_signal(barrier, inc=1, device_id=(peer, pcol), device_id_type=MESH)
        return carry

    def greet_col(i, carry):
        pl.semaphore_signal(
            barrier, inc=1, device_id=(prow, lax.rem(pcol + i, cols)), device_id_type=MESH
        )
        return carry

    lax.fori_loop(1, chips, greet_chip, 0)
    lax.fori_loop(1, cols, greet_col, 0)

    loads = {}
    for h in range(2):
        part = pl.ds(h * width, width)
        for level, (first, count) in enumerate(LEVELS):
            nodes = pl.ds(first, count)
            loads["rhs", h, level] = pltpu.make_async_copy(
                rhs_hbm.at[nodes, :, part], rhs.at[h, nodes], rhs_sem.at[h, level]
            )
    for k in range(SUPERNODES):
        loads["diag", k] = pltpu.make_async_copy(diag_hbm.at[k], diag.at[k], diag_sem.at[k])
        loads["panel", k] = pltpu.make_async_copy(panel_hbm.at[k], panel.at[k], panel_sem.at[k])
    loads["rhs", 0, 0].start()
    for k in range(4):
        loads["diag", k].start()
    loads["rhs", 1, 0].start()
    for k in range(4):
        loads["panel", k].start()
    for h in range(2):
        for level in (1, 2):
            loads["rhs", h, level].start()
    for k in range(4, SUPERNODES):
        loads["diag", k].start()
        loads["panel", k].start()

    def nodes_of(level):
        return pl.ds(*LEVELS[level])

    def each(level):
        first, count = LEVELS[level]
        return range(first, first + count)

    def split_diag(node):
        loads["diag", node].wait()
        diag_high[node], diag_low[node] = split(diag[node])

    def begin(level, h):
        for node in each(level):
            residual = rhs[h, node] if level == 0 else res[h, node - 4]
            r_high, r_low = split(residual)
            terms[h, node] = dot3(diag_high[node], diag_low[node], r_high, r_low)

    def pair(level, h):
        nodes = nodes_of(level)
        pltpu.make_async_remote_copy(
            src_ref=terms.at[h, nodes, pl.ds(other_half, BLOCK_ROWS)], dst_ref=pair_in.at[h, nodes],
            send_sem=pair_send.at[h, level], recv_sem=pair_recv.at[h, level],
            device_id=(other, pcol), device_id_type=MESH,
        ).start()
        sent.append((pair_in.at[h, nodes], pair_send.at[h, level]))

    def scatter(level, h):
        nodes = nodes_of(level)
        wait_bytes(pair_in.at[h, nodes], pair_recv.at[h, level])
        for node in each(level):
            half[h, node] = terms[h, node, pl.ds(own_half, BLOCK_ROWS)] + pair_in[h, node]

        def send(i, carry):
            peer = lax.rem(chip + i, chips)
            pltpu.make_async_remote_copy(
                src_ref=half.at[h, nodes, pl.ds(peer * rows, rows)], dst_ref=ring_in.at[h, i, nodes],
                send_sem=ring_send.at[h, level], recv_sem=ring_recv.at[h, level],
                device_id=(peer * 2 + core, pcol), device_id_type=MESH,
            ).start()
            return carry

        lax.fori_loop(1, chips, send, 0)
        sent.append((ring_in.at[h, pl.ds(1, chips - 1), nodes], ring_send.at[h, level]))

    def gather(level, h):
        nodes = nodes_of(level)
        wait_bytes(ring_in.at[h, pl.ds(1, chips - 1), nodes], ring_recv.at[h, level])
        for node in each(level):
            total = half[h, node, pl.ds(chip * rows, rows)]
            for i in range(1, chips):
                total = total + ring_in[h, i, node]
            xs[h, node, pl.ds(own_rows, rows)] = total
        here = xs.at[h, nodes, pl.ds(own_rows, rows)]

        def send(i, carry):
            peer = lax.rem(chip + i, chips)
            pltpu.make_async_remote_copy(
                src_ref=here, dst_ref=here,
                send_sem=gather_send.at[h, level], recv_sem=gather_recv.at[h, level],
                device_id=(peer * 2 + core, pcol), device_id_type=MESH,
            ).start()
            return carry

        lax.fori_loop(1, chips, send, 0)
        sent.append((ring_in.at[h, pl.ds(1, chips - 1), nodes], gather_send.at[h, level]))

    def share(level, h):
        nodes = nodes_of(level)
        wait_bytes(ring_in.at[h, pl.ds(1, chips - 1), nodes], gather_recv.at[h, level])
        here = xs.at[h, nodes, pl.ds(own_half, BLOCK_ROWS)]
        pltpu.make_async_remote_copy(
            src_ref=here, dst_ref=here,
            send_sem=share_send.at[h, level], recv_sem=share_recv.at[h, level],
            device_id=(other, pcol), device_id_type=MESH,
        ).start()
        sent.append((pair_in.at[h, nodes], share_send.at[h, level]))

    def multiply(level, h):
        wait_bytes(pair_in.at[h, nodes_of(level)], share_recv.at[h, level])
        for node in each(level):
            x_high, x_low = split(xs[h, node])
            product = dot3(panel_high[node], panel_low[node], x_high, x_low)
            for slot in range(8):
                prod[h, node, slot] = product[slot * BLOCK_ROWS:(slot + 1) * BLOCK_ROWS]

    def store(level, h):
        copy = pltpu.make_async_copy(
            xs.at[h, nodes_of(level)], sol_hbm.at[nodes_of(level), :, pl.ds(h * width, width)],
            out_sem.at[h, level],
        )
        copy.start()
        return copy

    def split_panel(node):
        loads["panel", node].wait()

        def one(step, carry):
            part = pl.ds(step * BLOCK_ROWS, BLOCK_ROWS)
            panel_high[node, part], panel_low[node, part] = split(panel[node, part])
            return carry

        lax.fori_loop(0, 8, one, 0)

    def picked(h, node, block):
        slot = 8
        for i in range(8):
            slot = jnp.where(rows_ref[node, i] == block, i, slot)
        return prod[h, node, slot]

    size = 2 * BLOCK_ROWS // cols
    windows = (pl.ds(0, 2), pl.ds(2, 1))
    targets = (((4, (0, 1)), (5, (2, 3))), ((6, (0, 1, 2, 3, 4, 5)),))

    def send_window(level, h):
        which = windows[level]
        for target, children in targets[level]:
            for b in range(2):
                block = target * super_blocks + prow * 2 + b
                total = picked(h, children[0], block)
                for node in children[1:]:
                    total = total + picked(h, node, block)
                win[h, target - 4, pl.ds(b * BLOCK_ROWS, BLOCK_ROWS)] = total

        def send(i, carry):
            peer = lax.rem(pcol + i, cols)
            pltpu.make_async_remote_copy(
                src_ref=win.at[h, which, pl.ds(peer * size, size)], dst_ref=win_in.at[h, i, which],
                send_sem=win_send.at[h, level], recv_sem=win_recv.at[h, level],
                device_id=(prow, peer), device_id_type=MESH,
            ).start()
            return carry

        lax.fori_loop(1, cols, send, 0)
        sent.append((win_in.at[h, pl.ds(1, cols - 1), which], win_send.at[h, level]))

    def spread(level, h):
        which = windows[level]
        loads["rhs", h, level + 1].wait()
        wait_bytes(win_in.at[h, pl.ds(1, cols - 1), which], win_recv.at[h, level])
        mine = pl.ds(pcol * size, size)
        for target, _ in targets[level]:
            total = win[h, target - 4, mine]
            for i in range(1, cols):
                total = total + win_in[h, i, target - 4]
            res[h, target - 4, mine] = rhs[h, target, mine] - total
        here = res.at[h, which, mine]

        def send(i, carry):
            pltpu.make_async_remote_copy(
                src_ref=here, dst_ref=here,
                send_sem=back_send.at[h, level], recv_sem=back_recv.at[h, level],
                device_id=(prow, lax.rem(pcol + i, cols)), device_id_type=MESH,
            ).start()
            return carry

        lax.fori_loop(1, cols, send, 0)
        sent.append((win_in.at[h, pl.ds(1, cols - 1), which], back_send.at[h, level]))

    def begin_next(level, h):
        wait_bytes(win_in.at[h, pl.ds(1, cols - 1), windows[level - 1]], back_recv.at[h, level - 1])
        begin(level, h)
        pair(level, h)

    def add_upper(which, h, nodes, fresh):
        count = upper.shape[4] // BLOCK_ROWS

        def one(j, carry):
            block = SUPERNODES * super_blocks + prow * 16 + j
            total = picked(h, nodes[0], block)
            for node in nodes[1:]:
                total = total + picked(h, node, block)
            place = j // count
            part = pl.ds((j % count) * BLOCK_ROWS, BLOCK_ROWS)
            spot = (which, h, place // side, place % side, part)
            upper[spot] = total if fresh else upper[spot] + total
            return carry

        lax.fori_loop(0, cols * count, one, 0)

    up_rows = upper.shape[4] // 2
    row_half = (pl.ds(0, up_rows), pl.ds(up_rows, up_rows))

    def send_upper(which, h):
        for i in range(1, side):
            peer_x, peer_y = lax.rem(col_x + i, side), lax.rem(col_y + i, side)
            pltpu.make_async_remote_copy(
                src_ref=upper.at[which, h, peer_x, :, row_half[0]], dst_ref=up_in.at[which, h, 0, i],
                send_sem=up_send.at[which, h, 0], recv_sem=up_recv.at[which, h, 0],
                device_id=(prow, peer_x * side + col_y), device_id_type=MESH,
            ).start()
            pltpu.make_async_remote_copy(
                src_ref=upper.at[which, h, :, peer_y, row_half[1]], dst_ref=up_in.at[which, h, 1, i],
                send_sem=up_send.at[which, h, 1], recv_sem=up_recv.at[which, h, 1],
                device_id=(prow, col_x * side + peer_y), device_id_type=MESH,
            ).start()
        for way in range(2):
            sent.append((up_in.at[which, h, way, pl.ds(1, side - 1)], up_send.at[which, h, way]))

    def middle_upper(which, h):
        for way in range(2):
            wait_bytes(up_in.at[which, h, way, pl.ds(1, side - 1)], up_recv.at[which, h, way])

            def one(j, carry):
                if way == 0:
                    total = upper[which, h, col_x, j, row_half[0]]
                else:
                    total = upper[which, h, j, col_y, row_half[1]]
                for i in range(1, side):
                    total = total + up_in[which, h, way, i, j]
                up_mid[which, h, way, j] = total
                return carry

            lax.fori_loop(0, side, one, 0)
            for i in range(1, side):
                if way == 0:
                    place = lax.rem(col_y + i, side)
                    peer = col_x * side + place
                else:
                    place = lax.rem(col_x + i, side)
                    peer = place * side + col_y
                pltpu.make_async_remote_copy(
                    src_ref=up_mid.at[which, h, way, place], dst_ref=up_last.at[which, h, way, i],
                    send_sem=last_send.at[which, h, way], recv_sem=last_recv.at[which, h, way],
                    device_id=(prow, peer), device_id_type=MESH,
                ).start()
            sent.append((up_last.at[which, h, way, pl.ds(1, side - 1)], last_send.at[which, h, way]))

    def finish_upper(which, h, fresh):
        for way in range(2):
            wait_bytes(up_last.at[which, h, way, pl.ds(1, side - 1)], last_recv.at[which, h, way])
            total = up_mid[which, h, way, col_y if way == 0 else col_x]
            for i in range(1, side):
                total = total + up_last[which, h, way, i]
            goal = (row_half[way], pl.ds(h * width, width))
            up_out[goal] = total if fresh else up_out[goal] + total

    def run():
        stores = []
        for h in range(2):
            loads["rhs", h, 0].wait()
            if h == 0:
                for node in range(4):
                    split_diag(node)
            begin(0, h)
            if h == 0:
                pl.semaphore_wait(barrier, chips + cols - 1)
            pair(0, h)
        yield
        for h in range(2):
            scatter(0, h)
        for h in range(2):
            for node in range(SUPERNODES):
                prod[h, node, 8] = jnp.zeros((BLOCK_ROWS, width), F32)
        for node in range(SUPERNODES):
            split_panel(node)
        for node in range(4, SUPERNODES):
            split_diag(node)
        yield
        for h in range(2):
            gather(0, h)
        yield
        for h in range(2):
            share(0, h)
            multiply(0, h)
            send_window(0, h)
        yield
        for h in range(2):
            spread(0, h)
        yield
        for h in range(2):
            stores.append(store(0, h))
            add_upper(0, h, (0, 1, 2, 3), True)
        for h in range(2):
            begin_next(1, h)
        yield
        for h in range(2):
            scatter(1, h)
        for h in range(2):
            send_upper(0, h)
        for h in range(2):
            gather(1, h)
        yield
        for h in range(2):
            share(1, h)
            multiply(1, h)
            send_window(1, h)
        yield
        for h in range(2):
            stores.append(store(1, h))
            add_upper(1, h, (4, 5), True)
        for h in range(2):
            spread(1, h)
        yield
        for h in range(2):
            begin_next(2, h)
        for h in range(2):
            scatter(2, h)
        for h in range(2):
            middle_upper(0, h)
        for h in range(2):
            gather(2, h)
        yield
        for h in range(2):
            share(2, h)
            multiply(2, h)
            add_upper(1, h, (6,), False)
            send_upper(1, h)
        yield
        for h in range(2):
            stores.append(store(2, h))
            finish_upper(0, h, True)
        for h in range(2):
            middle_upper(1, h)
        for h in range(2):
            finish_upper(1, h, False)
        last = pltpu.make_async_copy(up_out, up_hbm, out_sem.at[0, 3])
        last.start()
        for copy in stores:
            copy.wait()
        last.wait()

    for _ in run():
        pass
    for ref, sem in sent:
        wait_bytes(ref, sem)


def copy_out(sol_ref, up_ref, sol_out, up_out, sems):
    copies = [
        pltpu.make_async_copy(sol_ref.at[k], sol_out.at[k], sems.at[k]) for k in range(SUPERNODES)
    ]
    copies.append(pltpu.make_async_copy(up_ref, up_out, sems.at[SUPERNODES]))
    for copy in copies:
        copy.start()
    for copy in copies:
        copy.wait()


def per_device(chips, side, super_blocks, right_side, inverse_diag, panels, block_rows):
    rhs_cols = right_side.shape[2]
    order = right_side.shape[1]
    upper_own = 2 * block_rows.shape[1]
    rows = BLOCK_ROWS // chips
    cols = side * side
    own_upper = upper_own * BLOCK_ROWS // cols
    dma = pltpu.SemaphoreType.DMA
    width = rhs_cols // 2
    scratch = [
        pltpu.VMEM((2, 7, order, width), F32),
        pltpu.VMEM((7, order, order), F32),
        pltpu.VMEM((7, order, order), BF16),
        pltpu.VMEM((7, order, order), BF16),
        pltpu.VMEM(panels.shape, F32),
        pltpu.VMEM(panels.shape, BF16),
        pltpu.VMEM(panels.shape, BF16),
        pltpu.VMEM((2, 7, order, width), F32),
        pltpu.VMEM((2, 7, BLOCK_ROWS, width), F32),
        pltpu.VMEM((2, 7, BLOCK_ROWS, width), F32),
        pltpu.VMEM((2, chips, 7, rows, width), F32),
        pltpu.VMEM((2, 7, order, width), F32),
        pltpu.VMEM((2, 7, 9, BLOCK_ROWS, width), F32),
        pltpu.VMEM((2, 3, order, width), F32),
        pltpu.VMEM((2, cols, 3, order // cols, width), F32),
        pltpu.VMEM((2, 3, order, width), F32),
        pltpu.VMEM((2, 2, side, side, own_upper, width), F32),
        pltpu.VMEM((2, 2, 2, side, side, own_upper // 2, width), F32),
        pltpu.VMEM((2, 2, 2, side, own_upper // 2, width), F32),
        pltpu.VMEM((2, 2, 2, side, own_upper // 2, width), F32),
        pltpu.VMEM((own_upper, rhs_cols), F32),
        dma((2, 3)), dma((7,)), dma((7,)), dma((2, 3)), dma((2, 3)), dma((2, 3)), dma((2, 3)),
        dma((2, 3)), dma((2, 3)), dma((2, 3)), dma((2, 3)), dma((2, 2)), dma((2, 2)), dma((2, 2)), dma((2, 2)),
        dma((2, 2, 2)), dma((2, 2, 2)), dma((2, 2, 2)), dma((2, 2, 2)), dma((2, 4)),
    ]
    anywhere = pl.BlockSpec(memory_space=pl.ANY)
    stay = pl.BlockSpec(memory_space=pltpu.HBM)
    shapes = (
        jax.ShapeDtypeStruct((7, order, rhs_cols), F32),
        jax.ShapeDtypeStruct((own_upper, rhs_cols), F32),
    )
    results = pl.pallas_call(
        functools.partial(kernel, chips, side, super_blocks),
        out_shape=shapes,
        in_specs=[pl.BlockSpec(memory_space=pltpu.SMEM), stay, stay, stay],
        out_specs=(anywhere, anywhere),
        scratch_shapes=scratch,
        compiler_params=pltpu.CompilerParams(
            collective_id=0, has_side_effects=True, vmem_limit_bytes=52 * 1024 * 1024
        ),
    )(block_rows, right_side, inverse_diag, panels)
    return pl.pallas_call(
        copy_out,
        out_shape=shapes,
        in_specs=[pl.BlockSpec(memory_space=pltpu.VMEM)] * 2,
        out_specs=(stay, stay),
        scratch_shapes=[dma((8,))],
        compiler_params=pltpu.CompilerParams(vmem_limit_bytes=8 * 1024 * 1024),
    )(*results)


def solution(mesh):
    chips, side = mesh.shape["prow"] // 2, math.isqrt(mesh.shape["pcol"])
    super_blocks = 2 * mesh.shape["prow"]
    in_specs = (
        P(None, "prow", None),
        P(None, "pcol", "prow"),
        P(None, "prow", "pcol"),
        P(None, "prow"),
    )
    out_specs = (P(None, "pcol", None), P(("prow", "pcol"), None))
    return jax.shard_map(
        functools.partial(per_device, chips, side, super_blocks),
        mesh=mesh, in_specs=in_specs, out_specs=out_specs, check_vma=False,
    )
```

time: 123 us -> 120 us (0.976)
  Pallas kernels: 121 us -> 119 us
    pallas_call x1, Pallas kernels: 120 us -> 117 us  [per_device(): pl.pallas_call(functools.partial(kernel, chips, side, super_blocks), out_...]
where the time goes in v5:
time: 120 us
  Pallas kernels  119 us (99%)
    pallas_call x1, Pallas kernels, per_device(): pl.pallas_call(functools.partial(kernel, chips, side, super_blocks), out_...  117 us

profile of v5, /device:TPU:1, one launch (start us, length us, event | category | flops | bytes accessed | tf_op | source)
XLA Modules:
  0.0 119.8 jit_solution(15502248455331176790)
XLA Ops:
  0.6 0.0 copy-start
  0.6 0.7 copy-done
  1.3 117.2 %shard_map.59 = (f32[7,256,256]{2,1,0:T(8,128)S(1)}, f32[128,256]{1,0:T(8,128)S(1)}) custom-call(s32[7,8]{1,0:T(8,128)S(1)} %copy-done, f32[7,256,256]{2,1,0:T(8,128)} %rhs_hbm.1, f32[7,256,256]{2,1,0:T(8,128)} %diag_hbm.1, f32[7,1024,256]{2,1,0:T(8,128)} %panel_hbm.1), custom_call_target="tpu_custom_call" | custom-call | tf_op jit(solution)/shard_map/pallas_call | solution.py:475
  118.5 1.3 %shard_map.60 = (f32[7,256,256]{2,1,0:T(8,128)}, f32[128,256]{1,0:T(8,128)}) custom-call(f32[7,256,256]{2,1,0:T(8,128)S(1)} %get-tuple-element.4.sol_ref, f32[128,256]{1,0:T(8,128)S(1)} %get-tuple-element.5.up_ref), custom_call_target="tpu_custom_call" | custom-call | tf_op jit(solution)/shard_map/pallas_call | solution.py:485
Async XLA Ops:
  0.6 0.7 copy-start

commit v6 on v5

--- a/solution.py
+++ b/solution.py
@@ -25,7 +25,9 @@
 
 def dot3(a_high, a_low, b_high, b_low):
     dot = functools.partial(jnp.dot, preferred_element_type=F32)
-    return dot(a_high, b_high) + (dot(a_high, b_low) + dot(a_low, b_high))
+    width = b_high.shape[1]
+    both = dot(a_high, jnp.concatenate([b_high, b_low], axis=1))
+    return both[:, :width] + (both[:, width:] + dot(a_low, b_high))
 
 
 def wait_bytes(ref, sem):
@@ -329,6 +331,11 @@
             goal = (row_half[way], pl.ds(h * width, width))
             up_out[goal] = total if fresh else up_out[goal] + total
 
+    def drain(count):
+        for ref, sem in sent[:count]:
+            wait_bytes(ref, sem)
+        del sent[:count]
+
     def run():
         stores = []
         for h in range(2):
@@ -337,8 +344,8 @@
                 for node in range(4):
                     split_diag(node)
             begin(0, h)
-            if h == 0:
-                pl.semaphore_wait(barrier, chips + cols - 1)
+        pl.semaphore_wait(barrier, chips + cols - 1)
+        for h in range(2):
             pair(0, h)
         yield
         for h in range(2):
@@ -375,10 +382,12 @@
         for h in range(2):
             gather(1, h)
         yield
-        for h in range(2):
-            share(1, h)
-            multiply(1, h)
-            send_window(1, h)
+        share(1, 0)
+        multiply(1, 0)
+        share(1, 1)
+        send_window(1, 0)
+        multiply(1, 1)
+        send_window(1, 1)
         yield
         for h in range(2):
             stores.append(store(1, h))
@@ -397,6 +406,8 @@
         yield
         for h in range(2):
             share(2, h)
+        early = len(sent)
+        for h in range(2):
             multiply(2, h)
             add_upper(1, h, (6,), False)
             send_upper(1, h)
@@ -404,20 +415,20 @@
         for h in range(2):
             stores.append(store(2, h))
             finish_upper(0, h, True)
+        drain(early)
+        for copy in stores:
+            copy.wait()
         for h in range(2):
             middle_upper(1, h)
         for h in range(2):
             finish_upper(1, h, False)
         last = pltpu.make_async_copy(up_out, up_hbm, out_sem.at[0, 3])
         last.start()
-        for copy in stores:
-            copy.wait()
+        drain(len(sent))
         last.wait()
 
     for _ in run():
         pass
-    for ref, sem in sent:
-        wait_bytes(ref, sem)
 
 
 def copy_out(sol_ref, up_ref, sol_out, up_out, sems):

time: 120 us -> 118 us (0.983)
  Pallas kernels: 119 us -> 116 us
    pallas_call x1, Pallas kernels: 117 us -> 115 us  [per_device(): pl.pallas_call(functools.partial(kernel, chips, side, super_blocks), out_...]
where the time goes in v6:
time: 118 us
  Pallas kernels  116 us (98%)
    pallas_call x1, Pallas kernels, per_device(): pl.pallas_call(functools.partial(kernel, chips, side, super_blocks), out_...  115 us

profile of v6, /device:TPU:1, one launch (start us, length us, event | category | flops | bytes accessed | tf_op | source)
XLA Modules:
  0.0 117.5 jit_solution(6523208209985490999)
XLA Ops:
  0.6 0.0 copy-start
  0.6 0.7 copy-done
  1.3 114.8 %shard_map.59 = (f32[7,256,256]{2,1,0:T(8,128)S(1)}, f32[128,256]{1,0:T(8,128)S(1)}) custom-call(s32[7,8]{1,0:T(8,128)S(1)} %copy-done, f32[7,256,256]{2,1,0:T(8,128)} %rhs_hbm.1, f32[7,256,256]{2,1,0:T(8,128)} %diag_hbm.1, f32[7,1024,256]{2,1,0:T(8,128)} %panel_hbm.1), custom_call_target="tpu_custom_call" | custom-call | tf_op jit(solution)/shard_map/pallas_call | solution.py:486
  116.2 1.3 %shard_map.60 = (f32[7,256,256]{2,1,0:T(8,128)}, f32[128,256]{1,0:T(8,128)}) custom-call(f32[7,256,256]{2,1,0:T(8,128)S(1)} %get-tuple-element.4.sol_ref, f32[128,256]{1,0:T(8,128)S(1)} %get-tuple-element.5.up_ref), custom_call_target="tpu_custom_call" | custom-call | tf_op jit(solution)/shard_map/pallas_call | solution.py:496
Async XLA Ops:
  0.6 0.7 copy-start

commit v7 on v6

--- a/solution.py
+++ b/solution.py
@@ -95,6 +95,25 @@
         loads["diag", k].start()
         loads["panel", k].start()
 
+    def hops(i, count):
+        return min(i, count - i)
+
+    far_chips = sorted(range(1, chips), key=lambda i: -hops(i, chips))
+    far_cols = sorted(
+        range(1, cols), key=lambda i: -hops(i // side, side) - hops(i % side, side)
+    )
+
+    def col_peer(i):
+        return lax.rem(col_x + i // side, side) * side + lax.rem(col_y + i % side, side)
+
+    def to_chips(send):
+        for i in far_chips:
+            send(i, 0)
+
+    def to_cols(send):
+        for i in far_cols:
+            send(i, 0)
+
     def nodes_of(level):
         return pl.ds(*LEVELS[level])
 
@@ -136,7 +155,7 @@
             ).start()
             return carry
 
-        lax.fori_loop(1, chips, send, 0)
+        to_chips(send)
         sent.append((ring_in.at[h, pl.ds(1, chips - 1), nodes], ring_send.at[h, level]))
 
     def gather(level, h):
@@ -158,7 +177,7 @@
             ).start()
             return carry
 
-        lax.fori_loop(1, chips, send, 0)
+        to_chips(send)
         sent.append((ring_in.at[h, pl.ds(1, chips - 1), nodes], gather_send.at[h, level]))
 
     def share(level, h):
@@ -219,7 +238,7 @@
                 win[h, target - 4, pl.ds(b * BLOCK_ROWS, BLOCK_ROWS)] = total
 
         def send(i, carry):
-            peer = lax.rem(pcol + i, cols)
+            peer = col_peer(i)
             pltpu.make_async_remote_copy(
                 src_ref=win.at[h, which, pl.ds(peer * size, size)], dst_ref=win_in.at[h, i, which],
                 send_sem=win_send.at[h, level], recv_sem=win_recv.at[h, level],
@@ -227,7 +246,7 @@
             ).start()
             return carry
 
-        lax.fori_loop(1, cols, send, 0)
+        to_cols(send)
         sent.append((win_in.at[h, pl.ds(1, cols - 1), which], win_send.at[h, level]))
 
     def spread(level, h):
@@ -246,11 +265,11 @@
             pltpu.make_async_remote_copy(
                 src_ref=here, dst_ref=here,
                 send_sem=back_send.at[h, level], recv_sem=back_recv.at[h, level],
-                device_id=(prow, lax.rem(pcol + i, cols)), device_id_type=MESH,
+                device_id=(prow, col_peer(i)), device_id_type=MESH,
             ).start()
             return carry
 
-        lax.fori_loop(1, cols, send, 0)
+        to_cols(send)
         sent.append((win_in.at[h, pl.ds(1, cols - 1), which], back_send.at[h, level]))
 
     def begin_next(level, h):

time: 118 us -> 111 us (0.941)
  Pallas kernels: 116 us -> 109 us
    pallas_call x1, Pallas kernels: 115 us -> 108 us  [per_device(): pl.pallas_call(functools.partial(kernel, chips, side, super_blocks), out_...]
where the time goes in v7:
time: 111 us
  Pallas kernels  109 us (98%)
    pallas_call x1, Pallas kernels, per_device(): pl.pallas_call(functools.partial(kernel, chips, side, super_blocks), out_...  108 us

profile of v7, /device:TPU:1, one launch (start us, length us, event | category | flops | bytes accessed | tf_op | source)
XLA Modules:
  0.0 110.7 jit_solution(16185520618984313339)
XLA Ops:
  0.6 0.0 copy-start
  0.6 0.7 copy-done
  1.3 108.1 %shard_map.59 = (f32[7,256,256]{2,1,0:T(8,128)S(1)}, f32[128,256]{1,0:T(8,128)S(1)}) custom-call(s32[7,8]{1,0:T(8,128)S(1)} %copy-done, f32[7,256,256]{2,1,0:T(8,128)} %rhs_hbm.1, f32[7,256,256]{2,1,0:T(8,128)} %diag_hbm.1, f32[7,1024,256]{2,1,0:T(8,128)} %panel_hbm.1), custom_call_target="tpu_custom_call" | custom-call | tf_op jit(solution)/shard_map/pallas_call | solution.py:505
  109.4 1.3 %shard_map.60 = (f32[7,256,256]{2,1,0:T(8,128)}, f32[128,256]{1,0:T(8,128)}) custom-call(f32[7,256,256]{2,1,0:T(8,128)S(1)} %get-tuple-element.4.sol_ref, f32[128,256]{1,0:T(8,128)S(1)} %get-tuple-element.5.up_ref), custom_call_target="tpu_custom_call" | custom-call | tf_op jit(solution)/shard_map/pallas_call | solution.py:515
Async XLA Ops:
  0.6 0.7 copy-start

commit v8 on v7

--- a/solution.py
+++ b/solution.py
@@ -274,8 +274,15 @@
 
     def begin_next(level, h):
         wait_bytes(win_in.at[h, pl.ds(1, cols - 1), windows[level - 1]], back_recv.at[h, level - 1])
-        begin(level, h)
-        pair(level, h)
+        halves = [split(res[h, node - 4]) for node in each(level)]
+        for start in (other_half, own_half):
+            part = pl.ds(pl.multiple_of(start, BLOCK_ROWS), BLOCK_ROWS)
+            for node, (r_high, r_low) in zip(each(level), halves):
+                terms[h, node, part] = dot3(
+                    diag_high[node, part], diag_low[node, part], r_high, r_low
+                )
+            if start is other_half:
+                pair(level, h)
 
     def add_upper(which, h, nodes, fresh):
         count = upper.shape[4] // BLOCK_ROWS

time: 111 us -> 111 us (level)
  no operation moved by 1% of the time
where the time goes in v8:
time: 111 us
  Pallas kernels  110 us (99%)
    pallas_call x1, Pallas kernels, per_device(): pl.pallas_call(functools.partial(kernel, chips, side, super_blocks), out_...  108 us

profile of v8, /device:TPU:1, one launch (start us, length us, event | category | flops | bytes accessed | tf_op | source)
XLA Modules:
  0.0 110.9 jit_solution(8416595219829929908)
XLA Ops:
  0.6 0.0 copy-start
  0.6 0.7 copy-done
  1.3 108.3 %shard_map.59 = (f32[7,256,256]{2,1,0:T(8,128)S(1)}, f32[128,256]{1,0:T(8,128)S(1)}) custom-call(s32[7,8]{1,0:T(8,128)S(1)} %copy-done, f32[7,256,256]{2,1,0:T(8,128)} %rhs_hbm.1, f32[7,256,256]{2,1,0:T(8,128)} %diag_hbm.1, f32[7,1024,256]{2,1,0:T(8,128)} %panel_hbm.1), custom_call_target="tpu_custom_call" | custom-call | tf_op jit(solution)/shard_map/pallas_call | solution.py:512
  109.6 1.3 %shard_map.60 = (f32[7,256,256]{2,1,0:T(8,128)}, f32[128,256]{1,0:T(8,128)}) custom-call(f32[7,256,256]{2,1,0:T(8,128)S(1)} %get-tuple-element.4.sol_ref, f32[128,256]{1,0:T(8,128)S(1)} %get-tuple-element.5.up_ref), custom_call_target="tpu_custom_call" | custom-call | tf_op jit(solution)/shard_map/pallas_call | solution.py:522
Async XLA Ops:
  0.6 0.7 copy-start
